TPU v7x, 32 devices: a whole 2x2x4 slice. The times are simulated.
32 devices in a mesh: group: 2 (over x), tok: 16 (over z, y, core).
Axes of the slice: x: 2, y: 2, z: 4, core: 2. Of those that a mesh axis runs over, the one named last changes fastest.
Arguments:
- initial_guess: float32 [512, 16, 128], P(('group', 'tok')), parts along dimension 0, may hold values from -6 to 6
- noise_draws: float32 [512, 16, 128], P(('group', 'tok')), parts along dimension 0, may hold values from -6 to 6
- drift_state: float32 [16], replicated, may hold values from 0 to 0.15
- drift_denoise: float32 [16], replicated, may hold values from -0.4 to -0.15
- noise_scale: float32 [16], replicated, may hold values from 0.05 to 0.3
- modulation: float32 [16, 8, 1152], replicated, may hold values from -3 to 3
- embed_weight: bfloat16 [16, 1152], replicated, may hold values from -1.5 to 1.5
- space_input: bfloat16 [1152, 1728], replicated, may hold values from -0.1875 to 0.1875
- space_output: bfloat16 [576, 1152], replicated, may hold values from -0.25 to 0.25
- time_input: bfloat16 [1152, 1728], replicated, may hold values from -0.1875 to 0.1875
- time_output: bfloat16 [576, 1152], replicated, may hold values from -0.25 to 0.25
- final_weight: bfloat16 [1152, 16], replicated, may hold values from -0.1875 to 0.1875
Outputs:
- next_states: float32 [512, 16, 128], P(('group', 'tok')), parts along dimension 0
There are 2 independent parts, one for each index of `group`. A program takes and returns all parts, laid end to end along the dimension named above; an argument that names none is the same for every part. Nothing has to cross between parts.
All inputs are finite; a program needn't handle non-finite values.
Results may differ from a plain program's by a relative error of at most 0.006.
Values may be sent and summed in bfloat16 or wider, within the bound.
A program may use at most 128 MiB of HBM per device.

v0:
```python
import jax
import jax.numpy as jnp
from jax import lax
from jax.sharding import PartitionSpec as P

HEADS = 8
HD = 72
P_SIZE = 16
ITERS = 2


def carried_in(array, axis, join, neutral):
    place = lax.axis_index(axis)
    gathered = lax.all_gather(array.astype(jnp.bfloat16), axis)
    state = jnp.zeros_like(array) + jnp.asarray(neutral, array.dtype)

    def one(hop, state):
        return join(state, lax.dynamic_index_in_dim(gathered, hop, 0, False).astype(array.dtype))

    return lax.fori_loop(0, place, one, state)


def layer_norm(values):
    center = values - jnp.mean(values, -1, keepdims=True)
    return center * lax.rsqrt(jnp.mean(center * center, -1, keepdims=True) + 1e-06)


def head_norm(values):
    return values * lax.rsqrt(jnp.mean(values * values, -1, keepdims=True) + 1e-06)


def space_mix(normed, input_weight, output_weight):
    frames, length, feature_width = normed.shape
    packed = jnp.dot(
        normed.reshape(-1, feature_width), input_weight, preferred_element_type=jnp.float32
    )
    packed = packed.reshape(frames, length, 3, HEADS, HD)
    queries = head_norm(packed[:, :, 0]).astype(jnp.bfloat16)
    key_rows = head_norm(packed[:, :, 1]).astype(jnp.bfloat16)
    value_rows = packed[:, :, 2].astype(jnp.bfloat16)

    def one_frame(triple):
        query_frame, key_frame, value_frame = triple
        scores = jnp.einsum(
            "lhe,mhe->hlm", query_frame, key_frame, preferred_element_type=jnp.float32
        ) * HD ** (-0.5)
        weights = jnp.exp(scores)
        weights = (weights / jnp.sum(weights, -1, keepdims=True)).astype(jnp.bfloat16)
        return jnp.einsum(
            "hlm,mhe->lhe", weights, value_frame, preferred_element_type=jnp.float32
        ).astype(jnp.bfloat16)

    attended = lax.map(one_frame, (queries, key_rows, value_rows))
    result = jnp.dot(
        attended.reshape(-1, HEADS * HD), output_weight, preferred_element_type=jnp.float32
    )
    return result.reshape(frames, length, feature_width)


def time_mix(normed, input_weight, output_weight):
    timesteps, groups, frames, positions, feature_width = normed.shape
    packed = jnp.dot(
        normed.reshape(-1, feature_width), input_weight, preferred_element_type=jnp.float32
    )
    packed = packed.reshape(timesteps, groups, frames, positions, 3, HEADS, HD)
    queries = head_norm(packed[:, :, :, :, 0]).astype(jnp.bfloat16)
    key_rows = head_norm(packed[:, :, :, :, 1]).astype(jnp.bfloat16)
    value_rows = packed[:, :, :, :, 2].astype(jnp.bfloat16)
    scores = jnp.einsum(
        "pglnhe,pkmnhe->pnhglkm", queries, key_rows, preferred_element_type=jnp.float32
    ) * HD ** (-0.5)
    frame_count = groups * frames
    weights = jnp.exp(scores).reshape(timesteps, positions, HEADS, frame_count, frame_count)
    weights = (weights / jnp.sum(weights, -1, keepdims=True)).astype(jnp.bfloat16)
    weights = weights.reshape(timesteps, positions, HEADS, groups, frames, groups, frames)
    attended = jnp.einsum(
        "pnhglkm,pkmnhe->pglnhe", weights, value_rows, preferred_element_type=jnp.float32
    ).astype(jnp.bfloat16)
    result = jnp.dot(
        attended.reshape(-1, HEADS * HD), output_weight, preferred_element_type=jnp.float32
    )
    return result.reshape(timesteps, groups, frames, positions, feature_width)


def body(
    initial_guess,
    noise_draws,
    drift_state,
    drift_denoise,
    noise_scale,
    modulation,
    embed_weight,
    space_input,
    space_output,
    time_input,
    time_output,
    final_weight,
):
    frames_local, channels, spatial = initial_guess.shape
    model_width = embed_weight.shape[1]
    devices = lax.axis_size("tok")
    own_index = lax.axis_index("tok")
    groups = devices // P_SIZE
    timestep = own_index // groups
    block_index = own_index % groups
    positions = spatial // devices
    leading = timestep == 0
    modulation_row = lax.dynamic_index_in_dim(modulation, timestep, 0, keepdims=False)
    time_table = modulation.reshape(P_SIZE, 1, 1, 1, 8, model_width)
    rate_state = lax.dynamic_index_in_dim(drift_state, timestep, 0, keepdims=False)
    rate_denoise = lax.dynamic_index_in_dim(drift_denoise, timestep, 0, keepdims=False)
    rate_noise = lax.dynamic_index_in_dim(noise_scale, timestep, 0, keepdims=False)
    latent = initial_guess
    result = initial_guess
    for iteration in range(ITERS):
        embedded = jnp.einsum(
            "fch,cd->fhd",
            latent.astype(jnp.bfloat16),
            embed_weight,
            preferred_element_type=jnp.float32,
        )
        normed = (layer_norm(embedded) * (1.0 + modulation_row[1]) + modulation_row[0]).astype(
            jnp.bfloat16
        )
        after_space = (
            embedded + modulation_row[2] * space_mix(normed, space_input, space_output)
        ).astype(jnp.bfloat16)
        temporal = lax.all_to_all(after_space, "tok", split_axis=1, concat_axis=0, tiled=True)
        hidden = temporal.reshape(P_SIZE, groups, frames_local, positions, model_width).astype(
            jnp.float32
        )
        normed = (
            layer_norm(hidden) * (1.0 + time_table[:, :, :, :, 4]) + time_table[:, :, :, :, 3]
        ).astype(jnp.bfloat16)
        after_time = (
            hidden + time_table[:, :, :, :, 5] * time_mix(normed, time_input, time_output)
        ).astype(jnp.bfloat16)
        settled = lax.optimization_barrier(after_time).astype(jnp.float32)
        normed = (
            layer_norm(settled) * (1.0 + time_table[:, :, :, :, 7]) + time_table[:, :, :, :, 6]
        ).astype(jnp.bfloat16)
        outgoing = jnp.einsum(
            "pglnd,dc->pglcn", normed, final_weight, preferred_element_type=jnp.float32
        )
        outgoing = outgoing.reshape(devices * frames_local, channels, positions)
        predicted = lax.all_to_all(outgoing, "tok", split_axis=0, concat_axis=2, tiled=True)
        increment = rate_state * latent + rate_denoise * predicted + rate_noise * noise_draws
        increment = jnp.where(leading, increment + latent, increment)

        def combine(first_part, second_part):
            return first_part + second_part

        slot_mask = (jnp.arange(groups, dtype=jnp.int32) == block_index).astype(jnp.float32)
        slotted = slot_mask[:, None, None, None] * increment[None]
        scanned = carried_in(slotted, "tok", combine, jnp.zeros_like(slotted))
        before = lax.dynamic_index_in_dim(scanned, block_index, 0, keepdims=False)
        result = jnp.where(leading, 0.0, before) + increment
        latent = jnp.where(leading, latent, before)
    return result


def solution(mesh):
    placed = (
        P(("group", "tok"), None, None),
        P(("group", "tok"), None, None),
        P(),
        P(),
        P(),
        P(),
        P(),
        P(),
        P(),
        P(),
        P(),
        P(),
    )
    return jax.shard_map(
        body, mesh=mesh, in_specs=placed, out_specs=P(("group", "tok"), None, None), check_vma=False
    )
```

profile of v0, /device:TPU:29, one launch (start us, length us, event | category | flops | bytes accessed | tf_op | source)
XLA Modules:
  0.0 737.6 jit_solution(5119831308410877056)
XLA Ops:
  6.5 2.5 fusion.135
  10.2 2.5 copy-done.1
  13.3 14.0 %fusion.65 = f32[16,128,3,8,72]{1,4,3,2,0:T(8,128)S(1)} fusion(bf16[3,8,72,1152,1]{3,2,1,0,4:T(8,128)(2,1)} %bitcast.338, f32[16,128,1152]{2,1,0:T(8,128)} %copy-done.1, f32[1152]{0:T(1024)S(1)} %get-tuple-element.175, f32[1152]{0:T(1024)S(1)} %get-tuple-element.174, f32[16,128]{1,0:T(8,128)S(1)} %add_rsqrt_fusion.13, ...), kind=kOutput, calls=%fused_computation.97 | convolution fusion | flops 8165523456 | bytes 27599872 | tf_op jit(solution)/shard_map/dot_general | solution.py:34
  29.1 3.3 copy-done.4
  34.3 7.6 %multiply_convert_fusion.2 = (bf16[16,128,8,72]{1,3,2,0:T(8,128)(2,1)}, bf16[16,128,8,72]{1,3,2,0:T(8,128)(2,1)}) fusion(f32[16,128,3,8,72]{1,4,3,2,0:T(8,128)} %copy-done.4, f32[16,128,8]{1,2,0:T(8,128)S(1)} %get-tuple-element.235, f32[16,128,8]{1,2,0:T(8,128)S(1)} %get-tuple-element.236), kind=kLoop, calls=%fused_computation.126 | loop fusion | flops 4718592 | bytes 14286848 | tf_op jit(solution)/shard_map/convert_element_type | solution.py:39
  43.8 49.8 %while.40 = (s32[]{:T(128)}, bf16[16,128,8,72]{1,3,2,0:T(8,128)(2,1)}, bf16[16,128,8,72]{1,3,2,0:T(8,128)(2,1)}, bf16[16,128,8,72]{1,3,2,0:T(8,128)(2,1)}, bf16[16,128,8,72]{1,3,2,0:T(8,128)(2,1)}, /*index=5*/s32[]{:T(128)}) while((s32[]{:T(128)}, bf16[16,128,8,72]{1,3,2,0:T(8,128)(2,1)}, bf16[16,128,8,72]{1,3,2,0:T(8,128)(2,1)}, ...), condition=%wide.region_6.7_spmd, body=%wide.region_4.6_spmd.sunk | while | flops 38216832 | bytes 2164805 | solution.py:53
  93.5 8.0 %add_convert_fusion.4 = bf16[16,128,1152]{2,1,0:T(8,128)(2,1)S(1)} fusion(f32[16,128,1152]{2,1,0:T(8,128)} %copy-done.1, bf16[16,128,576]{1,2,0:T(8,128)(2,1)} %bitcast.324, f32[1152]{0:T(1024)S(1)} %get-tuple-element.173, bf16[576,1152]{1,0:T(8,128)(2,1)S(1)} %copy-done), kind=kOutput, calls=%fused_computation.71 | convolution fusion | flops 2724986880 | bytes 17846784 | tf_op jit(solution)/shard_map/dot_general | solution.py:54
  101.5 4.8 copy.200
  106.3 6.6 all-to-all-start
  113.4 102.2 %all-to-all-done = bf16[16,128,1152]{2,0,1:T(8,128)(2,1)} async-done(((bf16[16,128,1152]{2,0,1:T(8,128)(2,1)}), bf16[16,128,1152]{2,0,1:T(8,128)(2,1)}, u32[]{:S(2)}, u32[]{:S(2)}) %all-to-all-start) | async-done | bytes 4718624 | tf_op jit(solution)/shard_map/all_to_all | solution.py:128
  215.6 3.2 bitcast_reduce_fusion.1
  218.8 3.8 multiply_reduce_fusion.2
  222.7 22.4 %convolution_bitcast_fusion.1 = f32[16,1,16,8,3,8,72]{6,3,5,4,2,0,1:T(8,128)} fusion(bf16[3,8,72,1152,1,1]{3,2,1,0,5,4:T(8,128)(2,1)S(1)} %bitcast.340, f32[16,1152]{1,0:T(8,128)S(1)} %get-tuple-element.239, f32[16,1152]{1,0:T(8,128)S(1)} %get-tuple-element.240, f32[16,16,8]{2,1,0:T(8,128)S(1)} %add_rsqrt_fusion.7, ...), kind=kOutput, calls=%fused_computation.75 | convolution fusion | flops 8167882752 | bytes 23019520 | tf_op jit(solution)/shard_map/dot_general | solution.py:62
  245.1 8.6 %multiply_reduce_fusion.7 = (f32[16,16,8,8]{2,3,1,0:T(8,128)S(1)}, f32[16,16,8,8]{2,3,1,0:T(8,128)S(1)}) fusion(f32[16,1,16,8,3,8,72]{6,3,5,4,2,0,1:T(8,128)} %convolution_bitcast_fusion.1), kind=kLoop, calls=%fused_computation.93 | loop fusion | flops 4685824 | bytes 9568256 | tf_op jit(solution)/shard_map/reduce_sum | solution.py:29
  253.7 4.5 fusion.98
  258.5 7.5 %fusion.61 = (bf16[16,16,8,8,72]{4,2,3,1,0:T(8,128)(2,1)S(1)}, bf16[16,16,8,8,72]{4,2,3,1,0:T(8,128)(2,1)S(1)}) fusion(f32[16,1,16,8,3,8,72]{6,3,5,4,2,0,1:T(8,128)} %convolution_bitcast_fusion.1, f32[16,16,8,8]{2,3,1,0:T(8,128)S(1)} %add_rsqrt_fusion.3, f32[16,16,8,8]{2,3,1,0:T(8,128)S(1)} %add_rsqrt_fusion.2), kind=kLoop, calls=%fused_computation.85 | loop fusion | flops 4718592 | bytes 14286848 | tf_op jit(solution)/shard_map/convert_element_type | solution.py:66
  266.0 11.8 %fusion.62 = (f32[16,8,8,16]{3,2,1,0:T(8,128)S(1)}, f32[16,8,8,16,16]{3,4,2,1,0:T(8,128)}) fusion(bf16[16,16,8,8,72]{4,2,3,1,0:T(8,128)(2,1)S(1)} %get-tuple-element.217, bf16[16,16,8,8,72]{4,2,3,1,0:T(8,128)(2,1)S(1)} %get-tuple-element.216), kind=kOutput, calls=%fused_computation.94 | convolution fusion | flops 38256640 | bytes 5832704 | tf_op jit(solution)/shard_map/pglnhe,pkmnhe->pnhglkm/dot_general | solution.py:69
  277.8 6.0 convert_bitcast_fusion.1
  283.8 3.0 copy.207
  286.9 7.4 %dot_general.100 = bf16[16,16,8,576]{3,2,1,0:T(8,128)(2,1)} reshape(bf16[16,1,16,8,8,72]{5,4,3,2,0,1:T(8,128)(2,1)} %copy.207) | data formatting | bytes 4718592 | tf_op jit(solution)/shard_map/dot_general | solution.py:79
  294.3 7.9 %fusion.96 = bf16[16,1,16,8,1152]{4,3,2,0,1:T(8,128)(2,1)S(1)} fusion(bf16[16,16,8,576]{3,2,1,0:T(8,128)(2,1)} %dot_general.100, f32[16,1152]{1,0:T(8,128)S(1)} %bitcast.336, bf16[576,1152]{1,0:T(8,128)(2,1)S(1)} %copy-done.26, bf16[16,128,1152]{2,0,1:T(8,128)(2,1)} %all-to-all-done), kind=kOutput, calls=%fused_computation.138 | convolution fusion | flops 2727346176 | bytes 13197312 | tf_op jit(solution)/shard_map/dot_general | solution.py:79
  307.4 5.7 all-to-all-start.1
  315.1 2.4 all-to-all-done.1
  322.3 2.9 fusion.122
  325.2 37.0 %all-gather.5.cloned.1.call-done = bf16[256,16,128]{2,1,0:T(8,128)(2,1)} async-done(((bf16[16,16,128]{2,1,0:T(8,128)(2,1)}), bf16[256,16,128]{2,1,0:T(8,128)(2,1)}) %all-gather.5.cloned.1.call-update) | async-done | bytes 1048592 | tf_op jit(solution)/shard_map/all_gather | solution.py:14
  362.2 13.4 %while.41 = (s32[]{:T(128)}, f32[1,16,16,128]{3,2,1,0:T(8,128)S(1)}, s32[]{:T(128)}, bf16[16,1,16,16,128]{4,3,2,1,0:T(8,128)(2,1)}, s32[]{:T(128)}, /*index=5*/s32[]{:T(128)}, s32[]{:T(128)}) while((s32[]{:T(128)}, f32[1,16,16,128]{3,2,1,0:T(8,128)S(1)}, s32[]{:T(128)}, bf16[16,1,16,16,128]{4,3,2,1,0:T(8,128)(2,1)}, s32[]{:T(128)}, ...), condition=%wide.region_15.16_spmd, body=%wide.region_14.15_spmd.sunk | while | flops 65541 | bytes 327795 | solution.py:20
  375.7 2.3 fusion.136
  379.1 2.5 copy-done.2
  381.6 11.7 %fusion.70 = f32[16,128,3,8,72]{1,4,3,2,0:T(8,128)S(1)} fusion(bf16[3,8,72,1152,1]{3,2,1,0,4:T(8,128)(2,1)} %bitcast.339, f32[16,128,1152]{2,1,0:T(8,128)S(1)} %get-tuple-element.232, f32[16,128]{1,0:T(8,128)S(1)} %add_rsqrt_fusion.12, f32[16,128]{1,0:T(8,128)S(1)} %broadcast_multiply_fusion.6, f32[1152]{0:T(1024)S(1)} %copy-done.23, f32[1152]{0:T(1024)S(1)} %copy-done.21), kind=kOutput, calls=%fused_computation.100 | convolution fusion | flops 8165523456 | bytes 27599872 | tf_op jit(solution)/shard_map/dot_general | solution.py:34
  396.7 3.4 multiply_convert_fusion
  402.0 49.8 %while.42 = (s32[]{:T(128)}, bf16[16,128,8,72]{1,3,2,0:T(8,128)(2,1)}, bf16[16,128,8,72]{1,3,2,0:T(8,128)(2,1)}, bf16[16,128,8,72]{1,3,2,0:T(8,128)(2,1)}, bf16[16,128,8,72]{1,3,2,0:T(8,128)(2,1)}, /*index=5*/s32[]{:T(128)}) while((s32[]{:T(128)}, bf16[16,128,8,72]{1,3,2,0:T(8,128)(2,1)}, bf16[16,128,8,72]{1,3,2,0:T(8,128)(2,1)}, ...), condition=%wide.region_22.23_spmd, body=%wide.region_20.22_spmd.sunk | while | flops 38216832 | bytes 2164805 | solution.py:53
  451.8 8.4 %add_convert_fusion.1 = bf16[16,128,1152]{2,1,0:T(8,128)(2,1)S(1)} fusion(f32[16,128,1152]{2,1,0:T(8,128)} %copy-done.2, bf16[16,128,576]{1,2,0:T(8,128)(2,1)} %bitcast.323, f32[1152]{0:T(1024)S(1)} %copy-done.9, bf16[576,1152]{1,0:T(8,128)(2,1)S(1)} %copy-done), kind=kOutput, calls=%fused_computation.66 | convolution fusion | flops 2724986880 | bytes 17846784 | tf_op jit(solution)/shard_map/dot_general | solution.py:54
  460.2 2.7 copy.212
  462.9 108.5 %all_to_all.16 = bf16[16,128,1152]{2,0,1:T(8,128)(2,1)S(1)} all-to-all(bf16[16,128,1152]{2,0,1:T(8,128)(2,1)S(1)} %copy.212), channel_id=1, replica_groups=mesh['group'=2,'tok'=16] {'tok'}, dimensions={1} | all-to-all | bytes 9437184 | tf_op jit(solution)/shard_map/all_to_all | solution.py:128
  575.3 19.9 %convolution_bitcast_fusion = f32[16,1,16,8,3,8,72]{6,3,5,4,2,0,1:T(8,128)} fusion(bf16[3,8,72,1152,1,1]{3,2,1,0,5,4:T(8,128)(2,1)S(1)} %bitcast.341, f32[16,16,8]{2,1,0:T(8,128)S(1)} %add_rsqrt_fusion.5, f32[16,16,8]{2,1,0:T(8,128)S(1)} %broadcast_multiply_fusion.1, f32[16,1152]{1,0:T(8,128)S(1)} %copy-done.17, f32[16,1152]{1,0:T(8,128)S(1)} %copy-done.19, ...), kind=kOutput, calls=%fused_computation.74 | convolution fusion | flops 8167882752 | bytes 23019520 | tf_op jit(solution)/shard_map/dot_general | solution.py:62
  595.2 8.6 %multiply_reduce_fusion.5 = (f32[16,16,8,8]{2,3,1,0:T(8,128)S(1)}, f32[16,16,8,8]{2,3,1,0:T(8,128)S(1)}) fusion(f32[16,1,16,8,3,8,72]{6,3,5,4,2,0,1:T(8,128)} %convolution_bitcast_fusion), kind=kLoop, calls=%fused_computation.89 | loop fusion | flops 4685824 | bytes 9568256 | tf_op jit(solution)/shard_map/reduce_sum | solution.py:29
  603.8 6.5 fusion.99
  610.6 7.5 %fusion.59 = (bf16[16,16,8,8,72]{4,2,3,1,0:T(8,128)(2,1)S(1)}, bf16[16,16,8,8,72]{4,2,3,1,0:T(8,128)(2,1)S(1)}) fusion(f32[16,1,16,8,3,8,72]{6,3,5,4,2,0,1:T(8,128)} %convolution_bitcast_fusion, f32[16,16,8,8]{2,3,1,0:T(8,128)S(1)} %add_rsqrt_fusion.1, f32[16,16,8,8]{2,3,1,0:T(8,128)S(1)} %add_rsqrt_fusion), kind=kLoop, calls=%fused_computation.81 | loop fusion | flops 4718592 | bytes 14286848 | tf_op jit(solution)/shard_map/convert_element_type | solution.py:66
  618.0 11.6 %fusion.63 = (f32[16,8,8,16]{3,2,1,0:T(8,128)S(1)}, f32[16,8,8,16,16]{3,4,2,1,0:T(8,128)}) fusion(bf16[16,16,8,8,72]{4,2,3,1,0:T(8,128)(2,1)S(1)} %get-tuple-element.215, bf16[16,16,8,8,72]{4,2,3,1,0:T(8,128)(2,1)S(1)} %get-tuple-element.214), kind=kOutput, calls=%fused_computation.95 | convolution fusion | flops 38256640 | bytes 5832704 | tf_op jit(solution)/shard_map/pglnhe,pkmnhe->pnhglkm/dot_general | solution.py:69
  629.6 8.6 %convert_bitcast_fusion = bf16[16,1,16,8,8,72]{5,2,4,3,0,1:T(8,128)(2,1)S(1)} fusion(f32[16,8,8,16,16]{3,4,2,1,0:T(8,128)} %get-tuple-element.234, f32[16,8,8,16]{3,2,1,0:T(8,128)S(1)} %get-tuple-element.233, bf16[16,16,8,8,72]{4,2,3,1,0:T(8,128)(2,1)} %fusion.99), kind=kOutput, calls=%fused_computation.152 | convolution fusion | flops 39714816 | bytes 5832704 | tf_op jit(solution)/shard_map/pnhglkm,pkmnhe->pglnhe/dot_general | solution.py:76
  638.2 3.0 copy.219
  641.3 7.4 %dot_general.113 = bf16[16,16,8,576]{3,2,1,0:T(8,128)(2,1)} reshape(bf16[16,1,16,8,8,72]{5,4,3,2,0,1:T(8,128)(2,1)} %copy.219) | data formatting | bytes 4718592 | tf_op jit(solution)/shard_map/dot_general | solution.py:79
  648.7 8.0 %fusion.97 = bf16[16,1,16,8,1152]{4,3,2,0,1:T(8,128)(2,1)S(1)} fusion(bf16[16,16,8,576]{3,2,1,0:T(8,128)(2,1)} %dot_general.113, f32[16,1152]{1,0:T(8,128)S(1)} %bitcast.337, bf16[576,1152]{1,0:T(8,128)(2,1)S(1)} %copy-done.27, bf16[16,128,1152]{2,0,1:T(8,128)(2,1)} %copy-done.3), kind=kOutput, calls=%fused_computation.139 | convolution fusion | flops 2727346176 | bytes 13197312 | tf_op jit(solution)/shard_map/dot_general | solution.py:79
  661.1 9.9 %all_to_all.17 = f32[16,1,2048]{2,1,0:T(1,128)S(1)} all-to-all(f32[16,1,2048]{2,1,0:T(1,128)S(1)} %reshape.508), channel_id=1, replica_groups=mesh['group'=2,'tok'=16] {'tok'}, dimensions={0} | all-to-all | bytes 262144 | tf_op jit(solution)/shard_map/all_to_all | solution.py:146
  673.8 2.0 copy.221
  677.4 2.0 fusion.134
  679.3 37.1 %all-gather.7.cloned.1.call-done = bf16[256,16,128]{2,1,0:T(8,128)(2,1)} async-done(((bf16[16,16,128]{2,1,0:T(8,128)(2,1)}), bf16[256,16,128]{2,1,0:T(8,128)(2,1)}) %all-gather.7.cloned.1.call-update) | async-done | bytes 1048592 | tf_op jit(solution)/shard_map/all_gather | solution.py:14
  716.4 13.4 %while.43 = (s32[]{:T(128)}, f32[1,16,16,128]{3,2,1,0:T(8,128)S(1)}, s32[]{:T(128)}, bf16[16,1,16,16,128]{4,3,2,1,0:T(8,128)(2,1)}, s32[]{:T(128)}, /*index=5*/s32[]{:T(128)}, s32[]{:T(128)}) while((s32[]{:T(128)}, f32[1,16,16,128]{3,2,1,0:T(8,128)S(1)}, s32[]{:T(128)}, bf16[16,1,16,16,128]{4,3,2,1,0:T(8,128)(2,1)}, s32[]{:T(128)}, ...), condition=%wide.region_31.32_spmd, body=%wide.region_30.31_spmd.sunk | while | flops 65541 | bytes 327795 | solution.py:20
  (223 shorter events, 165.0 us)
Async XLA Ops:
  6.5 87.0 %copy-start = (bf16[576,1152]{1,0:T(8,128)(2,1)S(1)}, bf16[576,1152]{1,0:T(8,128)(2,1)}, u32[]{:S(2)}) copy-start(bf16[576,1152]{1,0:T(8,128)(2,1)} %param.28) | copy-start | bytes 3981316
  9.1 3.6 copy-start.1
  9.1 3.6 copy-start.7
  12.7 0.6 copy-start.20
  12.7 0.6 copy-start.22
  12.7 80.8 %copy-start.8 = (f32[1152]{0:T(1024)}, f32[1152]{0:T(1024)S(1)}, u32[]{:S(2)}) copy-start(f32[1152]{0:T(1024)S(1)} %get-tuple-element.173) | copy-start | bytes 13828
  27.3 5.1 copy-start.4
  106.3 109.2 %all-to-all-start = ((bf16[16,128,1152]{2,0,1:T(8,128)(2,1)}), bf16[16,128,1152]{2,0,1:T(8,128)(2,1)}, u32[]{:S(2)}, u32[]{:S(2)}) async-start(bf16[16,128,1152]{2,0,1:T(8,128)(2,1)} %copy.200), calls=%async_computation | async-start | bytes 9437184 | tf_op jit(solution)/shard_map/all_to_all | solution.py:128
  113.3 181.0 %copy-start.10 = (f32[16,1,1,1,1,1152]{5,0,4,3,2,1:T(8,128)}, f32[16,1,1,1,1,1152]{5,0,4,3,2,1:T(8,128)S(1)}, u32[]{:S(2)}) copy-start(f32[16,1,1,1,1,1152]{5,0,4,3,2,1:T(8,128)S(1)} %copy.299) | copy-start | bytes 221188
  113.3 109.3 %copy-start.16 = (f32[16,1152]{1,0:T(8,128)}, f32[16,1152]{1,0:T(8,128)S(1)}, u32[]{:S(2)}) copy-start(f32[16,1152]{1,0:T(8,128)S(1)} %get-tuple-element.239) | copy-start | bytes 221188
  113.3 109.3 %copy-start.18 = (f32[16,1152]{1,0:T(8,128)}, f32[16,1152]{1,0:T(8,128)S(1)}, u32[]{:S(2)}) copy-start(f32[16,1152]{1,0:T(8,128)S(1)} %get-tuple-element.240) | copy-start | bytes 221188
  113.4 191.0 %copy-start.12 = (f32[16,1152]{1,0:T(8,128)}, f32[16,1152]{1,0:T(8,128)S(1)}, u32[]{:S(2)}) copy-start(f32[16,1152]{1,0:T(8,128)S(1)} %get-tuple-element.237) | copy-start | bytes 221188
  113.4 191.0 %copy-start.14 = (f32[16,1152]{1,0:T(8,128)}, f32[16,1152]{1,0:T(8,128)S(1)}, u32[]{:S(2)}) copy-start(f32[16,1152]{1,0:T(8,128)S(1)} %get-tuple-element.238) | copy-start | bytes 221188
  215.6 7.1 copy-start.24
  286.9 7.4 %copy-start.26 = (bf16[576,1152]{1,0:T(8,128)(2,1)S(1)}, bf16[576,1152]{1,0:T(8,128)(2,1)}, u32[]{:S(2)}) copy-start(bf16[576,1152]{1,0:T(8,128)(2,1)} %param.30) | copy-start | bytes 3981316
  302.2 2.2 copy-start.28
  304.4 8.8 %copy-start.30 = (f32[16]{0:T(128)S(1)}, f32[16]{0:T(128)}, u32[]{:S(2)}) copy-start(f32[16]{0:T(128)} %param.23) | copy-start | bytes 196
  304.4 9.4 %copy-start.31 = (f32[16]{0:T(128)S(1)}, f32[16]{0:T(128)}, u32[]{:S(2)}) copy-start(f32[16]{0:T(128)} %param.22) | copy-start | bytes 196
  304.4 10.1 %copy-start.32 = (f32[16]{0:T(128)S(1)}, f32[16]{0:T(128)}, u32[]{:S(2)}) copy-start(f32[16]{0:T(128)} %param.24) | copy-start | bytes 196
  306.4 15.9 %copy-start.5 = (f32[16,16,128]{2,1,0:T(8,128)S(1)}, f32[16,16,128]{2,1,0:T(8,128)}, u32[]{:S(2)}) copy-start(f32[16,16,128]{2,1,0:T(8,128)} %param.20) | copy-start | bytes 393220
  307.4 10.1 %all-to-all-start.1 = ((f32[16,1,2048]{2,1,0:T(1,128)}), f32[16,1,2048]{2,1,0:T(1,128)S(1)}, u32[]{:S(2)}, u32[]{:S(2)}) async-start(f32[16,1,2048]{2,1,0:T(1,128)} %reshape.506), calls=%async_computation.1 | async-start | bytes 262144 | tf_op jit(solution)/shard_map/all_to_all | solution.py:146
  313.1 49.1 %all-gather.5.cloned.1.call-start = ((), (), s32[]{:S(2)}) async-start(), calls=%async_computation.4 | async-start | bytes 1114112 | tf_op jit(solution)/shard_map/all_gather | solution.py:14
  325.1 391.3 %all-gather.7.cloned.1.call-start = ((), (), s32[]{:S(2)}) async-start(), calls=%async_computation.5 | async-start | bytes 1114112 | tf_op jit(solution)/shard_map/all_gather | solution.py:14
  378.0 3.6 copy-start.2
  378.0 3.6 copy-start.21
  378.0 3.6 copy-start.23
  402.0 49.8 %copy-start.9 = (f32[1152]{0:T(1024)S(1)}, f32[1152]{0:T(1024)}, u32[]{:S(2)}) copy-start(f32[1152]{0:T(1024)} %copy-done.8) | copy-start | bytes 13828
  571.4 2.6 copy-start.3
  571.4 2.6 copy-start.17
  571.4 2.6 copy-start.19
  571.4 3.9 copy-start.25
  641.3 7.4 %copy-start.11 = (f32[16,1,1,1,1,1152]{5,0,4,3,2,1:T(8,128)S(1)}, f32[16,1,1,1,1,1152]{5,0,4,3,2,1:T(8,128)}, u32[]{:S(2)}) copy-start(f32[16,1,1,1,1,1152]{5,0,4,3,2,1:T(8,128)} %copy-done.10) | copy-start | bytes 221188
  641.3 7.4 %copy-start.27 = (bf16[576,1152]{1,0:T(8,128)(2,1)S(1)}, bf16[576,1152]{1,0:T(8,128)(2,1)}, u32[]{:S(2)}) copy-start(bf16[576,1152]{1,0:T(8,128)(2,1)} %param.30) | copy-start | bytes 3981316
  656.7 2.2 copy-start.13
  656.7 2.2 copy-start.15
  656.7 2.2 copy-start.29
  660.7 16.6 %copy-start.6 = (f32[16,16,128]{2,1,0:T(8,128)S(1)}, f32[16,16,128]{2,1,0:T(8,128)}, u32[]{:S(2)}) copy-start(f32[16,16,128]{2,1,0:T(8,128)} %param.21) | copy-start | bytes 393220
Sparse Core Ops, SparseCore 0:
  325.3 36.9 all-gather.4
  679.5 36.8 all-gather.6
where the time goes:
time: 744 us; the launch traced here: 738 us
  matrix products  246 us (33%)
  waiting for transfers between devices  179 us (24%)
  blocking collectives  118 us (16%)
  other arithmetic  98.4 us (13%)
  local copies, waits for them, and re-layouts  68 us (9%)
  between operations  14.4 us (2%)
  starting transfers between devices  12.5 us (2%)
    all_to_all x1, blocking collectives, body(): lax.all_to_all(after_space, 'tok', split_axis=1, concat_axis=0, tiled=True)  109 us
    all_to_all x1, waiting for transfers between devices, body(): lax.all_to_all(after_space, 'tok', split_axis=1, concat_axis=0, tiled=True)  102 us
    all_gather x2, waiting for transfers between devices, carried_in(): gathered = lax.all_gather(array.astype(jnp.bfloat16), axis)  74.1 us
    dot_general x32, matrix products, one_frame(): jnp.einsum('hlm,mhe->lhe', weights, value_frame, preferred_element_type=j...  58.8 us
    dot_general x2, matrix products, time_mix(): jnp.dot(normed.reshape(-1, feature_width), input_weight, preferred_elemen...  42.2 us
    dot_general x32, matrix products, one_frame(): jnp.einsum('lhe,mhe->hlm', query_frame, key_frame, preferred_element_type...  40.5 us
    add x30, other arithmetic, combine(): return first_part + second_part  26 us
    dot_general x2, matrix products, space_mix(): jnp.dot(normed.reshape(-1, feature_width), input_weight, preferred_elemen...  25.7 us
  transfers between devices with their start and end apart: 4, of which 4 were waited for; matrix products, arithmetic and copies ran while one was open for 0% of the time, Pallas kernels for 0%

commit v1 on v0

v1 whole, which is shorter than its diff:
```python
import functools
import math

import jax
import jax.numpy as jnp
from jax import lax
from jax.experimental import pallas as pl
from jax.experimental.pallas import tpu as pltpu
from jax.sharding import PartitionSpec as P

HEADS = 8
HD = 72
P_SIZE = 16
ITERS = 2
LANES = 128
INNER = HEADS * HD
PADDED = -(-INNER // LANES) * LANES
BLOCK_TOKENS = 256


def layer_norm(values):
    center = values - jnp.mean(values, -1, keepdims=True)
    return center * lax.rsqrt(jnp.mean(center * center, -1, keepdims=True) + 1e-06)


def head_slab(head):
    first = head * HD // LANES
    last = (head * HD + HD - 1) // LANES
    return first, last - first + 1


def attend(read, write, rows, keep):
    lane = lax.broadcasted_iota(jnp.int32, (rows, LANES), 1)
    outs = []
    for head in range(HEADS):
        tile, tiles = head_slab(head)
        low = head * HD - tile * LANES
        width = tiles * LANES
        lanes = lax.broadcasted_iota(jnp.int32, (rows, width), 1)
        inside = (lanes >= low) & (lanes < low + HD)
        queries = jnp.where(inside, read(0, tile, tiles), 0.0)
        keys = jnp.where(inside, read(1, tile, tiles), 0.0)
        values = read(2, tile, tiles).astype(jnp.bfloat16)
        query_rate = lax.rsqrt(jnp.sum(queries * queries, -1, keepdims=True) / HD + 1e-06)
        key_rate = lax.rsqrt(jnp.sum(keys * keys, -1, keepdims=True) / HD + 1e-06)
        queries = (queries * (query_rate * (HD**-0.5 * math.log2(math.e)))).astype(jnp.bfloat16)
        keys = (keys * key_rate).astype(jnp.bfloat16)
        scores = lax.dot_general(
            queries, keys, (((1,), (1,)), ((), ())), preferred_element_type=jnp.float32
        )
        weights = jnp.exp2(scores)
        if keep is not None:
            weights = jnp.where(keep, weights, 0.0)
        weights = weights * (1.0 / jnp.sum(weights, -1, keepdims=True))
        outs.append(
            jnp.dot(weights.astype(jnp.bfloat16), values, preferred_element_type=jnp.float32)
        )
    for tile in range(PADDED // LANES):
        total = None
        for head in range(HEADS):
            first, tiles = head_slab(head)
            if first <= tile < first + tiles:
                part = outs[head][:, (tile - first) * LANES : (tile - first + 1) * LANES]
                if total is None:
                    total = part
                else:
                    total = jnp.where(lane >= head * HD - tile * LANES, part, total)
        write(tile, total)


def space_kernel(
    latent_ref, table_ref, embed_ref, input_ref, output_ref, after_ref,
    embedded_ref, packed_ref, mixed_ref,
):
    frames, channels, spatial = latent_ref.shape
    for frame in range(frames):
        embedded_ref[frame * spatial : (frame + 1) * spatial, :] = lax.dot_general(
            latent_ref[frame].astype(jnp.bfloat16),
            embed_ref[...],
            (((0,), (0,)), ((), ())),
            preferred_element_type=jnp.float32,
        )
    normed = (
        layer_norm(embedded_ref[...]) * (1.0 + table_ref[1:2, :]) + table_ref[0:1, :]
    ).astype(jnp.bfloat16)
    packed_ref[...] = jnp.dot(normed, input_ref[...], preferred_element_type=jnp.float32)

    def one(frame, carry):
        rows = pl.ds(pl.multiple_of(frame * spatial, spatial), spatial)

        def read(part, tile, tiles):
            return packed_ref[rows, part * PADDED + tile * LANES : part * PADDED + (tile + tiles) * LANES]

        def write(tile, values):
            mixed_ref[rows, tile * LANES : (tile + 1) * LANES] = values

        attend(read, write, spatial, None)
        return carry

    lax.fori_loop(0, frames, one, 0)
    result = jnp.dot(
        mixed_ref[...].astype(jnp.bfloat16), output_ref[...], preferred_element_type=jnp.float32
    )
    after = (embedded_ref[...] + table_ref[2:3, :] * result).astype(jnp.bfloat16)
    after_ref[...] = after.reshape(after_ref.shape)


def time_kernel(
    after_ref, table_ref, input_ref, output_ref, final_ref, predicted_ref, packed_ref, mixed_ref
):
    frames, positions, width = after_ref.shape
    chunk = 8
    tokens = frames * positions
    rows = frames * chunk
    hidden = after_ref[...].reshape(tokens, width).astype(jnp.float32)
    normed = (layer_norm(hidden) * (1.0 + table_ref[4:5, :]) + table_ref[3:4, :]).astype(
        jnp.bfloat16
    )
    packed_ref[...] = jnp.dot(
        normed, input_ref[...], preferred_element_type=jnp.float32
    ).reshape(packed_ref.shape)
    keep = (lax.broadcasted_iota(jnp.int32, (rows, rows), 0) % chunk) == (
        lax.broadcasted_iota(jnp.int32, (rows, rows), 1) % chunk
    )

    def one(index, carry):
        own = pl.ds(pl.multiple_of(index * chunk, chunk), chunk)

        def read(part, tile, tiles):
            block = packed_ref[
                :, own, part * PADDED + tile * LANES : part * PADDED + (tile + tiles) * LANES
            ]
            return block.reshape(rows, tiles * LANES)

        def write(tile, values):
            mixed_ref[:, own, tile * LANES : (tile + 1) * LANES] = values.reshape(
                frames, chunk, LANES
            )

        attend(read, write, rows, keep)
        return carry

    lax.fori_loop(0, positions // chunk, one, 0)
    mixed = mixed_ref[...].reshape(tokens, PADDED).astype(jnp.bfloat16)
    result = jnp.dot(mixed, output_ref[...], preferred_element_type=jnp.float32)
    hidden = after_ref[...].reshape(tokens, width).astype(jnp.float32)
    settled = (hidden + table_ref[5:6, :] * result).astype(jnp.bfloat16).astype(jnp.float32)
    normed = (layer_norm(settled) * (1.0 + table_ref[7:8, :]) + table_ref[6:7, :]).astype(
        jnp.bfloat16
    )
    predicted = jnp.dot(normed, final_ref[...], preferred_element_type=jnp.float32)
    predicted_ref[...] = predicted.reshape(predicted_ref.shape)


def whole(array):
    zeros = (0,) * array.ndim
    return pl.BlockSpec(array.shape, lambda step: zeros, pipeline_mode=pl.Buffered(1))


def space_block(latent, table, embed_weight, input_weight, output_weight):
    frames, channels, spatial = latent.shape
    width = embed_weight.shape[1]
    step_frames = math.gcd(frames, max(1, BLOCK_TOKENS // spatial))
    tokens = step_frames * spatial
    return pl.pallas_call(
        space_kernel,
        grid=(frames // step_frames,),
        out_shape=jax.ShapeDtypeStruct((frames, spatial, width), jnp.bfloat16),
        in_specs=[
            pl.BlockSpec((step_frames, channels, spatial), lambda step: (step, 0, 0)),
            whole(table),
            whole(embed_weight),
            whole(input_weight),
            whole(output_weight),
        ],
        out_specs=pl.BlockSpec((step_frames, spatial, width), lambda step: (step, 0, 0)),
        scratch_shapes=[
            pltpu.VMEM((tokens, width), jnp.float32),
            pltpu.VMEM((tokens, 3 * PADDED), jnp.float32),
            pltpu.VMEM((tokens, PADDED), jnp.float32),
        ],
        compiler_params=pltpu.CompilerParams(vmem_limit_bytes=40 * 1024 * 1024),
        name="space_block",
    )(latent, table, embed_weight, input_weight, output_weight)


def time_block(after, table, input_weight, output_weight, final_weight):
    frames, positions, width = after.shape
    channels = final_weight.shape[1]
    step_positions = math.gcd(positions, max(16, BLOCK_TOKENS // frames))
    return pl.pallas_call(
        time_kernel,
        grid=(positions // step_positions,),
        out_shape=jax.ShapeDtypeStruct((frames, positions, channels), jnp.float32),
        in_specs=[
            pl.BlockSpec((frames, step_positions, width), lambda step: (0, step, 0)),
            whole(table),
            whole(input_weight),
            whole(output_weight),
            whole(final_weight),
        ],
        out_specs=pl.BlockSpec((frames, step_positions, channels), lambda step: (0, step, 0)),
        scratch_shapes=[
            pltpu.VMEM((frames, step_positions, 3 * PADDED), jnp.float32),
            pltpu.VMEM((frames, step_positions, PADDED), jnp.float32),
        ],
        compiler_params=pltpu.CompilerParams(vmem_limit_bytes=40 * 1024 * 1024),
        name="time_block",
    )(after, table, input_weight, output_weight, final_weight)


def pad_input(weight):
    width = weight.shape[0]
    parts = weight.reshape(width, 3, INNER)
    return jnp.pad(parts, ((0, 0), (0, 0), (0, PADDED - INNER))).reshape(width, 3 * PADDED)


def pad_output(weight):
    return jnp.pad(weight, ((0, PADDED - INNER), (0, 0)))


def body(
    initial_guess,
    noise_draws,
    drift_state,
    drift_denoise,
    noise_scale,
    modulation,
    embed_weight,
    space_input,
    space_output,
    time_input,
    time_output,
    final_weight,
):
    devices = lax.axis_size("tok")
    own_index = lax.axis_index("tok")
    groups = devices // P_SIZE
    timestep = own_index // groups
    leading = timestep == 0
    table = lax.dynamic_index_in_dim(modulation, timestep, 0, keepdims=False)
    rate_state = lax.dynamic_index_in_dim(drift_state, timestep, 0, keepdims=False)
    rate_denoise = lax.dynamic_index_in_dim(drift_denoise, timestep, 0, keepdims=False)
    rate_noise = lax.dynamic_index_in_dim(noise_scale, timestep, 0, keepdims=False)
    space_in, space_out = pad_input(space_input), pad_output(space_output)
    time_in, time_out = pad_input(time_input), pad_output(time_output)
    same_step = [[step * groups + block for block in range(groups)] for step in range(P_SIZE)]
    same_block = [[step * groups + block for step in range(P_SIZE)] for block in range(groups)]
    latent = initial_guess
    result = initial_guess
    for iteration in range(ITERS):
        after = space_block(latent, table, embed_weight, space_in, space_out)
        if groups > 1:
            after = lax.all_to_all(
                after, "tok", split_axis=1, concat_axis=0, axis_index_groups=same_step, tiled=True
            )
        predicted = time_block(after, table, time_in, time_out, final_weight)
        predicted = jnp.swapaxes(predicted, 1, 2)
        if groups > 1:
            predicted = lax.all_to_all(
                predicted, "tok", split_axis=0, concat_axis=2, axis_index_groups=same_step, tiled=True
            )
        increment = rate_state * latent + rate_denoise * predicted + rate_noise * noise_draws
        increment = jnp.where(leading, increment + latent, increment)
        gathered = lax.all_gather(
            increment.astype(jnp.bfloat16),
            "tok",
            axis_index_groups=same_block if groups > 1 else None,
        )
        earlier = (jnp.arange(P_SIZE) < timestep)[:, None, None, None]
        before = jnp.sum(jnp.where(earlier, gathered.astype(jnp.float32), 0.0), axis=0)
        result = before + increment
        latent = jnp.where(leading, latent, before)
    return result


def solution(mesh):
    placed = (
        P(("group", "tok"), None, None),
        P(("group", "tok"), None, None),
        P(),
        P(),
        P(),
        P(),
        P(),
        P(),
        P(),
        P(),
        P(),
        P(),
    )
    return jax.shard_map(
        body, mesh=mesh, in_specs=placed, out_specs=P(("group", "tok"), None, None), check_vma=False
    )
```

time: 744 us -> 357 us (0.48)
  matrix products: 246 us -> 0 us
  Pallas kernels: 0 us -> 192 us
  blocking collectives: 118 us -> 0 us
  waiting for transfers between devices: 179 us -> 74.2 us
  other arithmetic: 98.4 us -> 13.8 us
  starting transfers between devices: 12.5 us -> 0.22 us
  local copies, waits for them, and re-layouts: 68 us -> 58.1 us
    dot_general x80 -> x0, matrix products: 246 us -> none  [the longest x32 58.8 us: one_frame(): jnp.einsum('hlm,mhe->lhe', weights, value_frame, preferred_element_type=j...]
    pallas_call x0 -> x4, Pallas kernels: none -> 192 us  [the longest x2 99.6 us: time_block(): pl.pallas_call(time_kernel, grid=(positions // step_positions,), out_shap...]
    all_to_all x2 -> x0, blocking collectives: 118 us -> none  [the longest x1 109 us: body(): lax.all_to_all(after_space, 'tok', split_axis=1, concat_axis=0, tiled=True)]
    all_to_all x2 -> x0, waiting for transfers between devices: 105 us -> none  [the longest x1 102 us: body(): lax.all_to_all(after_space, 'tok', split_axis=1, concat_axis=0, tiled=True)]
    reduce_sum x14 -> x2, other arithmetic: 36.4 us -> 3.67 us  [body(): jnp.sum(jnp.where(earlier, gathered.astype(jnp.float32), 0.0), axis=0)]
    convert_element_type x6 -> x0, other arithmetic: 30.8 us -> none  [the longest x2 15 us: time_mix(): queries = head_norm(packed[:, :, :, :, 0]).astype(jnp.bfloat16)]
    convert_element_type x8 -> x0, local copies, waits for them, and re-layouts: 28.2 us -> none  [the longest x2 11 us: time_mix(): value_rows = packed[:, :, :, :, 2].astype(jnp.bfloat16)]
    add x32 -> x1, other arithmetic: 27 us -> 1.11 us  [body(): result = before + increment]
  transfers between devices with their start and end apart: 4 -> 2, of which waited for: 4 -> 2; matrix products, arithmetic and copies ran while one was open for 0% -> 0% of each run, Pallas kernels for 0% -> 0%
where the time goes in v1:
time: 357 us; the launch traced here: 352 us
  Pallas kernels  192 us (54%)
  waiting for transfers between devices  74.2 us (21%)
  local copies, waits for them, and re-layouts  58.1 us (16%)
  other arithmetic  13.8 us (4%)
  between operations  13.6 us (4%)
    pallas_call x2, Pallas kernels, time_block(): pl.pallas_call(time_kernel, grid=(positions // step_positions,), out_shap...  99.6 us
    pallas_call x2, Pallas kernels, space_block(): pl.pallas_call(space_kernel, grid=(frames // step_frames,), out_shape=jax...  92.4 us
    all_gather x2, waiting for transfers between devices, body(): lax.all_gather(increment.astype(jnp.bfloat16), 'tok', axis_index_groups=s...  74.1 us
    unnamed x51, local copies, waits for them, and re-layouts  20 us
    reshape x2, local copies, waits for them, and re-layouts, pad_input(): jnp.pad(parts, ((0, 0), (0, 0), (0, PADDED - INNER)))  13.3 us
    pad x2, local copies, waits for them, and re-layouts, pad_input(): jnp.pad(parts, ((0, 0), (0, 0), (0, PADDED - INNER)))  9.2 us
  transfers between devices with their start and end apart: 2, of which 2 were waited for; matrix products, arithmetic and copies ran while one was open for 0% of the time, Pallas kernels for 0%

profile of v1, /device:TPU:29, one launch (start us, length us, event | category | flops | bytes accessed | tf_op | source)
XLA Modules:
  0.0 351.9 jit_solution(16490650205283448550)
XLA Ops:
  6.5 4.6 %pad.14 = bf16[1152,3,640]{0,2,1:T(8,128)(2,1)} pad(bf16[1152,3,576]{0,2,1:T(8,128)(2,1)} %bitcast.27, bf16[]{:T(256)} %constant.32.clone.1), padding=0_0x0_0x0_64 | pad | bytes 8404994 | tf_op jit(solution)/shard_map/jit(_pad)/pad | solution.py:215
  11.2 6.7 %copy.70.input_ref = bf16[1152,1920]{1,0:T(8,128)(2,1)} copy(bf16[1152,1920]{0,1:T(8,128)(2,1)} %bitcast.25) | data formatting | bytes 8847360 | tf_op jit(solution)/shard_map/reshape | solution.py:215
  17.8 0.1 pad.15.output_ref
  17.9 4.6 %pad.16 = bf16[1152,3,640]{0,2,1:T(8,128)(2,1)} pad(bf16[1152,3,576]{0,2,1:T(8,128)(2,1)} %bitcast.28, bf16[]{:T(256)} %constant.32.clone.1), padding=0_0x0_0x0_64 | pad | bytes 8404994 | tf_op jit(solution)/shard_map/jit(_pad)/pad | solution.py:215
  22.5 6.6 %copy.71.input_ref = bf16[1152,1920]{1,0:T(8,128)(2,1)} copy(bf16[1152,1920]{0,1:T(8,128)(2,1)} %bitcast.26) | data formatting | bytes 8847360 | tf_op jit(solution)/shard_map/reshape | solution.py:215
  29.1 1.4 pad.17.output_ref
  30.6 0.0 copy-start.22
  30.6 0.0 copy-start.23
  30.6 1.7 copy.72.final_ref
  32.3 0.6 dynamic-slice_bitcast_fusion.table_ref
  32.9 0.6 dynamic_slice.14
  33.5 2.2 copy.77
  35.7 2.2 broadcast_multiply_fusion
  37.9 2.2 copy.73
  40.1 0.6 dynamic_slice.15
  40.7 0.6 dynamic_slice.17
  41.2 2.2 copy.74
  43.5 2.3 copy-done.1
  45.7 0.9 copy-done.7
  46.6 0.8 copy-done.8
  47.4 0.8 copy-done.13
  48.1 46.2 %space_block.2.after_ref = bf16[16,128,1152]{2,1,0:T(8,128)(2,1)S(1)} custom-call(f32[16,16,128]{2,1,0:T(8,128)S(1)} %copy-done.7, f32[8,1152]{1,0:T(8,128)S(1)} %copy-done.8, bf16[16,1152]{1,0:T(8,128)(2,1)S(1)} %copy-done.13, bf16[1152,1920]{1,0:T(8,128)(2,1)S(1)} %copy-done.1, bf16[640,1152]{1,0:T(8,128)(2,1)S(1)} %pad.15.output_ref), custom_call_target="tpu_custom_call" | custom-call | tf_op jit(solution)/shard_map/space_block/pallas_call | solution.py:165
  94.4 2.2 copy-done.3
  96.7 49.8 %time_block.2 = f32[16,128,16]{2,1,0:T(8,128)S(1)} custom-call(bf16[16,128,1152]{2,1,0:T(8,128)(2,1)S(1)} %space_block.2.after_ref, f32[8,1152]{1,0:T(8,128)S(1)} %copy-done.9, bf16[1152,1920]{1,0:T(8,128)(2,1)S(1)} %copy-done.3, bf16[640,1152]{1,0:T(8,128)(2,1)S(1)} %pad.17.output_ref, bf16[1152,16]{1,0:T(8,128)(2,1)S(1)} %copy-done.5), custom_call_target="tpu_custom_call" | custom-call | tf_op jit(solution)/shard_map/time_block/pallas_call | solution.py:191
  146.5 2.4 add_select_fusion.1
  148.9 1.8 copy.76
  150.7 0.0 all-gather.5.cloned.1.call-update
  150.7 0.2 all-gather.7.cloned.1.call-start
  151.0 37.1 %all-gather.5.cloned.1.call-done = bf16[256,16,128]{2,1,0:T(8,128)(2,1)} async-done(((bf16[16,16,128]{2,1,0:T(8,128)(2,1)}), bf16[256,16,128]{2,1,0:T(8,128)(2,1)}) %all-gather.5.cloned.1.call-update) | async-done | bytes 1048592 | tf_op jit(solution)/shard_map/all_gather | solution.py:265
  188.1 2.2 fusion.1
  190.3 2.2 copy.78
  192.5 2.3 broadcast_select_fusion
  194.8 2.2 copy.79.latent_ref
  197.0 2.3 copy-done.2
  199.2 0.8 copy-done.10
  200.0 0.9 copy-done.12
  200.9 0.8 copy-done.14
  201.7 46.2 %space_block.3.after_ref = bf16[16,128,1152]{2,1,0:T(8,128)(2,1)S(1)} custom-call(f32[16,16,128]{2,1,0:T(8,128)S(1)} %copy-done.12, f32[8,1152]{1,0:T(8,128)S(1)} %copy-done.10, bf16[16,1152]{1,0:T(8,128)(2,1)S(1)} %copy-done.14, bf16[1152,1920]{1,0:T(8,128)(2,1)S(1)} %copy-done.2, bf16[640,1152]{1,0:T(8,128)(2,1)S(1)} %pad.15.output_ref), custom_call_target="tpu_custom_call" | custom-call | tf_op jit(solution)/shard_map/space_block/pallas_call | solution.py:165
  248.0 2.2 copy-done.4
  250.2 49.8 %time_block.3 = f32[16,128,16]{2,1,0:T(8,128)S(1)} custom-call(bf16[16,128,1152]{2,1,0:T(8,128)(2,1)S(1)} %space_block.3.after_ref, f32[8,1152]{1,0:T(8,128)S(1)} %copy-done.11, bf16[1152,1920]{1,0:T(8,128)(2,1)S(1)} %copy-done.4, bf16[640,1152]{1,0:T(8,128)(2,1)S(1)} %pad.17.output_ref, bf16[1152,16]{1,0:T(8,128)(2,1)S(1)} %copy-done.6), custom_call_target="tpu_custom_call" | custom-call | tf_op jit(solution)/shard_map/time_block/pallas_call | solution.py:191
  300.0 2.1 add_select_fusion
  302.1 0.8 copy.83
  303.0 0.0 all-gather.7.cloned.1.call-update
  303.0 37.0 %all-gather.7.cloned.1.call-done = bf16[256,16,128]{2,1,0:T(8,128)(2,1)} async-done(((bf16[16,16,128]{2,1,0:T(8,128)(2,1)}), bf16[256,16,128]{2,1,0:T(8,128)(2,1)}) %all-gather.7.cloned.1.call-update) | async-done | bytes 1048592 | tf_op jit(solution)/shard_map/all_gather | solution.py:265
  340.0 1.5 fusion
  341.5 0.3 copy.84
  341.8 1.1 add.45
  342.9 2.2 copy.85
  (38 shorter events, 0.1 us)
Async XLA Ops:
  6.5 25.7 %copy-start = (f32[16,8,1152]{2,1,0:T(8,128)S(1)}, f32[16,8,1152]{2,1,0:T(8,128)}, u32[]{:S(2)}) copy-start(f32[16,8,1152]{2,1,0:T(8,128)} %param.17) | copy-start | bytes 1769476
  6.5 181.6 %all-gather.5.cloned.1.call-start = ((), (), s32[]{:S(2)}) async-start(), calls=%async_computation | async-start | bytes 1114112 | tf_op jit(solution)/shard_map/all_gather | solution.py:265
  11.1 6.7 %copy-start.20 = (bf16[576,1152]{1,0:T(8,128)(2,1)S(1)}, bf16[576,1152]{1,0:T(8,128)(2,1)}, u32[]{:S(2)}) copy-start(bf16[576,1152]{1,0:T(8,128)(2,1)} %param.20) | copy-start | bytes 3981316
  29.1 3.8 %copy-start.21 = (f32[16]{0:T(128)S(1)}, f32[16]{0:T(128)}, u32[]{:S(2)}) copy-start(f32[16]{0:T(128)} %param.14) | copy-start | bytes 196
  30.6 9.5 %copy-start.22 = (f32[16]{0:T(128)S(1)}, f32[16]{0:T(128)}, u32[]{:S(2)}) copy-start(f32[16]{0:T(128)} %param.15) | copy-start | bytes 196
  30.6 10.1 %copy-start.23 = (f32[16]{0:T(128)S(1)}, f32[16]{0:T(128)}, u32[]{:S(2)}) copy-start(f32[16]{0:T(128)} %param.16) | copy-start | bytes 196
  43.4 2.3 copy-start.1
  45.7 0.9 copy-start.7
  46.6 0.8 copy-start.8
  47.4 0.8 copy-start.13
  48.1 46.2 %copy-start.5 = (bf16[1152,16]{1,0:T(8,128)(2,1)S(1)}, bf16[1152,16]{1,0:T(8,128)(2,1)}, u32[]{:S(2)}) copy-start(bf16[1152,16]{1,0:T(8,128)(2,1)} %copy.72.final_ref) | copy-start | bytes 110596
  48.1 46.2 %copy-start.9 = (f32[8,1152]{1,0:T(8,128)S(1)}, f32[8,1152]{1,0:T(8,128)}, u32[]{:S(2)}) copy-start(f32[8,1152]{1,0:T(8,128)} %dynamic-slice_bitcast_fusion.table_ref) | copy-start | bytes 110596
  94.4 2.3 copy-start.3
  96.7 49.8 %copy-start.15 = (f32[16,16,128]{1,2,0:T(8,128)S(1)}, f32[16,16,128]{1,2,0:T(8,128)}, u32[]{:S(2)}) copy-start(f32[16,16,128]{1,2,0:T(8,128)} %copy.77) | copy-start | bytes 393220
  96.7 49.8 %copy-start.17 = (f32[16,16,128]{1,2,0:T(8,128)S(1)}, f32[16,16,128]{1,2,0:T(8,128)}, u32[]{:S(2)}) copy-start(f32[16,16,128]{1,2,0:T(8,128)} %copy.74) | copy-start | bytes 393220
  96.7 49.8 %copy-start.19 = (f32[16,16,128]{1,2,0:T(8,128)S(1)}, f32[16,16,128]{1,2,0:T(8,128)}, u32[]{:S(2)}) copy-start(f32[16,16,128]{1,2,0:T(8,128)} %copy.73) | copy-start | bytes 393220
  150.7 189.2 %all-gather.7.cloned.1.call-start = ((), (), s32[]{:S(2)}) async-start(), calls=%async_computation.1 | async-start | bytes 1114112 | tf_op jit(solution)/shard_map/all_gather | solution.py:265
  197.0 2.3 copy-start.2
  199.2 0.8 copy-start.10
  200.0 0.9 copy-start.12
  200.9 0.8 copy-start.14
  201.7 46.2 %copy-start.6 = (bf16[1152,16]{1,0:T(8,128)(2,1)S(1)}, bf16[1152,16]{1,0:T(8,128)(2,1)}, u32[]{:S(2)}) copy-start(bf16[1152,16]{1,0:T(8,128)(2,1)} %copy.72.final_ref) | copy-start | bytes 110596
  201.7 46.2 %copy-start.11 = (f32[8,1152]{1,0:T(8,128)S(1)}, f32[8,1152]{1,0:T(8,128)}, u32[]{:S(2)}) copy-start(f32[8,1152]{1,0:T(8,128)} %dynamic-slice_bitcast_fusion.table_ref) | copy-start | bytes 110596
  247.9 2.3 copy-start.4
  250.2 49.8 %copy-start.16 = (f32[16,16,128]{1,2,0:T(8,128)S(1)}, f32[16,16,128]{1,2,0:T(8,128)}, u32[]{:S(2)}) copy-start(f32[16,16,128]{1,2,0:T(8,128)} %broadcast_select_fusion) | copy-start | bytes 393220
  250.2 49.8 %copy-start.18 = (f32[16,16,128]{1,2,0:T(8,128)S(1)}, f32[16,16,128]{1,2,0:T(8,128)}, u32[]{:S(2)}) copy-start(f32[16,16,128]{1,2,0:T(8,128)} %copy.74) | copy-start | bytes 393220
Sparse Core Ops, SparseCore 0:
  150.8 37.2 all-gather.4
  303.1 36.8 all-gather.6

commit v2 on v1

v2 whole, which is shorter than its diff:
```python
import functools
import math

import jax
import jax.numpy as jnp
from jax import lax
from jax.experimental import pallas as pl
from jax.experimental.pallas import tpu as pltpu
from jax.sharding import PartitionSpec as P

HEADS = 8
HD = 72
P_SIZE = 16
ITERS = 2
LANES = 128
INNER = HEADS * HD
PADDED = -(-INNER // LANES) * LANES
BLOCK_TOKENS = 256
SIDE = math.isqrt(P_SIZE)


def layer_norm(values):
    center = values - jnp.mean(values, -1, keepdims=True)
    return center * lax.rsqrt(jnp.mean(center * center, -1, keepdims=True) + 1e-06)


def head_slab(head):
    first = head * HD // LANES
    last = (head * HD + HD - 1) // LANES
    return first, last - first + 1


def part_lanes(part, tile, tiles):
    if part == 1:
        return 1, tile * LANES, (tile + tiles) * LANES
    start = part * INNER
    return 0, start + tile * LANES, start + min((tile + tiles) * LANES, INNER if part else PADDED)


def lined_keys(packed):
    low = INNER // LANES * LANES
    return pltpu.roll(packed[:, low : low + PADDED], PADDED - (INNER - low), 1)


def attend(read, write, rows, keep):
    lane = lax.broadcasted_iota(jnp.int32, (rows, LANES), 1)
    outs = []
    for head in range(HEADS):
        tile, tiles = head_slab(head)
        low = head * HD - tile * LANES
        width = tiles * LANES
        lanes = lax.broadcasted_iota(jnp.int32, (rows, width), 1)
        inside = (lanes >= low) & (lanes < low + HD)
        queries = jnp.where(inside, read(0, tile, tiles), 0.0)
        keys = jnp.where(inside, read(1, tile, tiles), 0.0)
        values = read(2, tile, tiles).astype(jnp.bfloat16)
        query_rate = lax.rsqrt(jnp.sum(queries * queries, -1, keepdims=True) / HD + 1e-06)
        key_rate = lax.rsqrt(jnp.sum(keys * keys, -1, keepdims=True) / HD + 1e-06)
        queries = (queries * (query_rate * (HD**-0.5 * math.log2(math.e)))).astype(jnp.bfloat16)
        keys = (keys * key_rate).astype(jnp.bfloat16)
        scores = lax.dot_general(
            queries, keys, (((1,), (1,)), ((), ())), preferred_element_type=jnp.float32
        )
        weights = jnp.exp2(scores)
        if keep is not None:
            weights = jnp.where(keep, weights, 0.0)
        weights = weights * (1.0 / jnp.sum(weights, -1, keepdims=True))
        outs.append(
            jnp.dot(weights.astype(jnp.bfloat16), values, preferred_element_type=jnp.float32)
        )
    for tile in range(PADDED // LANES):
        total = None
        for head in range(HEADS):
            first, tiles = head_slab(head)
            if first <= tile < first + tiles:
                part = outs[head][:, (tile - first) * LANES : (tile - first + 1) * LANES]
                if total is None:
                    total = part
                else:
                    total = jnp.where(lane >= head * HD - tile * LANES, part, total)
        write(tile, total)


def space_kernel(
    step_ref, latent_ref, table_ref, embed_ref, input_ref, output_ref, after_ref,
    embedded_ref, packed_ref, key_ref, mixed_ref,
):
    frames, channels, spatial = latent_ref.shape
    for frame in range(frames):
        embedded_ref[frame * spatial : (frame + 1) * spatial, :] = lax.dot_general(
            latent_ref[frame].astype(jnp.bfloat16),
            embed_ref[...],
            (((0,), (0,)), ((), ())),
            preferred_element_type=jnp.float32,
        )
    normed = (
        layer_norm(embedded_ref[...]) * (1.0 + table_ref[1:2, :]) + table_ref[0:1, :]
    ).astype(jnp.bfloat16)
    packed = jnp.dot(normed, input_ref[...], preferred_element_type=jnp.float32)
    packed_ref[...] = packed
    key_ref[...] = lined_keys(packed)

    def one(frame, carry):
        rows = pl.ds(pl.multiple_of(frame * spatial, spatial), spatial)

        def read(part, tile, tiles):
            source, start, stop = part_lanes(part, tile, tiles)
            return (packed_ref, key_ref)[source][rows, start:stop]

        def write(tile, values):
            mixed_ref[rows, tile * LANES : tile * LANES + values.shape[1]] = values

        attend(read, write, spatial, None)
        return carry

    lax.fori_loop(0, frames, one, 0)
    result = jnp.dot(
        mixed_ref[...].astype(jnp.bfloat16), output_ref[...], preferred_element_type=jnp.float32
    )
    after = (embedded_ref[...] + table_ref[2:3, :] * result).astype(jnp.bfloat16)
    after_ref[...] = after.reshape(after_ref.shape)


def time_kernel(fused, *refs):
    step_ref, after_ref, table_ref, input_ref, output_ref, final_ref, *refs = refs
    if fused:
        latent_ref, noise_ref, *rate_refs, increment_ref, sent_ref = refs[:7]
    else:
        result_ref = refs[0]
    predicted_ref, packed_ref, key_ref, mixed_ref = refs[-4:]
    frames, positions, width = after_ref.shape
    chunk = 8
    tokens = frames * positions
    rows = frames * chunk
    hidden = after_ref[...].reshape(tokens, width).astype(jnp.float32)
    normed = (layer_norm(hidden) * (1.0 + table_ref[4:5, :]) + table_ref[3:4, :]).astype(
        jnp.bfloat16
    )
    packed = jnp.dot(normed, input_ref[...], preferred_element_type=jnp.float32)
    packed_ref[...] = packed.reshape(packed_ref.shape)
    key_ref[...] = lined_keys(packed).reshape(key_ref.shape)
    keep = (lax.broadcasted_iota(jnp.int32, (rows, rows), 0) % chunk) == (
        lax.broadcasted_iota(jnp.int32, (rows, rows), 1) % chunk
    )

    def one(index, carry):
        own = pl.ds(pl.multiple_of(index * chunk, chunk), chunk)

        def read(part, tile, tiles):
            source, start, stop = part_lanes(part, tile, tiles)
            return (packed_ref, key_ref)[source][:, own, start:stop].reshape(rows, stop - start)

        def write(tile, values):
            lanes = values.shape[1]
            mixed_ref[:, own, tile * LANES : tile * LANES + lanes] = values.reshape(
                frames, chunk, lanes
            )

        attend(read, write, rows, keep)
        return carry

    lax.fori_loop(0, positions // chunk, one, 0)
    mixed = mixed_ref[...].reshape(tokens, INNER).astype(jnp.bfloat16)
    result = jnp.dot(mixed, output_ref[...], preferred_element_type=jnp.float32)
    hidden = after_ref[...].reshape(tokens, width).astype(jnp.float32)
    settled = (hidden + table_ref[5:6, :] * result).astype(jnp.bfloat16).astype(jnp.float32)
    normed = (layer_norm(settled) * (1.0 + table_ref[7:8, :]) + table_ref[6:7, :]).astype(
        jnp.bfloat16
    )
    predicted = jnp.dot(normed, final_ref[...], preferred_element_type=jnp.float32)
    own = pl.ds(pl.multiple_of(pl.program_id(0) * positions, positions), positions)
    predicted_ref[:, own, :] = predicted.reshape(frames, positions, predicted.shape[1])

    @pl.when(pl.program_id(0) == pl.num_programs(0) - 1)
    def _():
        if fused:
            timestep = step_ref[0]
            rate_state, rate_denoise, rate_noise = (ref[timestep] for ref in rate_refs)
            rate_state = rate_state + jnp.where(timestep == 0, 1.0, 0.0)
        for frame in range(frames):
            turned = predicted_ref[frame].T
            if fused:
                turned = (
                    rate_state * latent_ref[frame]
                    + rate_denoise * turned
                    + rate_noise * noise_ref[frame]
                )
                increment_ref[frame] = turned
                sent_ref[frame] = turned.astype(jnp.bfloat16)
            else:
                result_ref[frame] = turned


def whole(array):
    zeros = (0,) * array.ndim
    return pl.BlockSpec(array.shape, lambda step, *_: zeros, pipeline_mode=pl.Buffered(1))


def own_row(modulation):
    return pl.BlockSpec(
        (None,) + modulation.shape[1:],
        lambda step, own: (own[0], 0, 0),
        pipeline_mode=pl.Buffered(1),
    )


def cost_of(tokens, *weights):
    return pl.CostEstimate(
        flops=2 * tokens * sum(weight.size for weight in weights),
        bytes_accessed=2 * sum(weight.size for weight in weights) + 4 * tokens * weights[0].shape[0],
        transcendentals=0,
    )


def space_block(own, latent, modulation, embed_weight, input_weight, output_weight):
    frames, channels, spatial = latent.shape
    width = embed_weight.shape[1]
    step_frames = math.gcd(frames, max(1, BLOCK_TOKENS // spatial))
    tokens = step_frames * spatial
    return pl.pallas_call(
        space_kernel,
        out_shape=jax.ShapeDtypeStruct((frames, spatial, width), jnp.bfloat16),
        grid_spec=pltpu.PrefetchScalarGridSpec(
            num_scalar_prefetch=1,
            grid=(frames // step_frames,),
            in_specs=[
                pl.BlockSpec((step_frames, channels, spatial), lambda step, own: (step, 0, 0)),
                own_row(modulation),
                whole(embed_weight),
                whole(input_weight),
                whole(output_weight),
            ],
            out_specs=pl.BlockSpec((step_frames, spatial, width), lambda step, own: (step, 0, 0)),
            scratch_shapes=[
                pltpu.VMEM((tokens, width), jnp.float32),
                pltpu.VMEM((tokens, 3 * INNER), jnp.float32),
                pltpu.VMEM((tokens, PADDED), jnp.float32),
                pltpu.VMEM((tokens, INNER), jnp.float32),
            ],
        ),
        compiler_params=pltpu.CompilerParams(vmem_limit_bytes=36 * 1024 * 1024),
        cost_estimate=cost_of(frames * spatial, input_weight, output_weight, output_weight),
        name="space_block",
    )(own, latent, modulation, embed_weight, input_weight, output_weight)


def time_block(own, after, modulation, input_weight, output_weight, final_weight, fused=()):
    frames, positions, width = after.shape
    channels = final_weight.shape[1]
    step_positions = math.gcd(positions, max(16, BLOCK_TOKENS // frames))
    shape = (frames, channels, positions)
    kinds = [jnp.float32] + [jnp.bfloat16] * bool(fused)
    return pl.pallas_call(
        functools.partial(time_kernel, bool(fused)),
        out_shape=[jax.ShapeDtypeStruct(shape, kind) for kind in kinds],
        grid_spec=pltpu.PrefetchScalarGridSpec(
            num_scalar_prefetch=1,
            grid=(positions // step_positions,),
            in_specs=[
                pl.BlockSpec((frames, step_positions, width), lambda step, own: (0, step, 0)),
                own_row(modulation),
                whole(input_weight),
                whole(output_weight),
                whole(final_weight),
            ]
            + [
                whole(array) if array.ndim > 1 else pl.BlockSpec(memory_space=pltpu.SMEM)
                for array in fused
            ],
            out_specs=[
                pl.BlockSpec(shape, lambda step, own: (0, 0, 0), pipeline_mode=pl.Buffered(1))
                for kind in kinds
            ],
            scratch_shapes=[
                pltpu.VMEM((frames, positions, channels), jnp.float32),
                pltpu.VMEM((frames, step_positions, 3 * INNER), jnp.float32),
                pltpu.VMEM((frames, step_positions, PADDED), jnp.float32),
                pltpu.VMEM((frames, step_positions, INNER), jnp.float32),
            ],
        ),
        compiler_params=pltpu.CompilerParams(vmem_limit_bytes=36 * 1024 * 1024),
        cost_estimate=cost_of(frames * positions, input_weight, output_weight, output_weight),
        name="time_block",
    )(own, after, modulation, input_weight, output_weight, final_weight, *fused)


def carry_kernel(
    last, groups, sent_ref, increment_ref, latent_ref, out_ref,
    part_ref, total_ref, plane_ref, early_ref, stage_ref, before_ref,
    part_send, part_recv, plane_send, plane_recv, stage_send, stage_recv,
):
    quarter = part_ref.shape[1]
    own = lax.axis_index("tok")
    timestep = own // groups
    plane, seat = timestep // SIDE, timestep % SIDE

    def device(plane, seat):
        return {"tok": (plane * SIDE + seat) * groups + own % groups}

    def seat_after(hop):
        return (seat + hop) % SIDE

    barrier = pltpu.get_barrier_semaphore()
    for hop in range(1, SIDE):
        for target in (device(plane, seat_after(hop)), device((plane + hop) % SIDE, seat)):
            pl.semaphore_signal(
                barrier, inc=1, device_id=target, device_id_type=pl.DeviceIdType.MESH
            )
    pl.semaphore_wait(barrier, 2 * (SIDE - 1))

    def copy(source, target, send, receive, to):
        return pltpu.make_async_remote_copy(
            src_ref=source,
            dst_ref=target,
            send_sem=send,
            recv_sem=receive,
            device_id=to,
            device_id_type=pl.DeviceIdType.MESH,
        )

    def rows_of(index):
        return pl.ds(pl.multiple_of(index * quarter, quarter), quarter)

    parts = []
    for hop in range(1, SIDE):
        seat_to = seat_after(hop)
        parts.append(
            copy(
                sent_ref.at[rows_of(seat_to)], part_ref.at[hop - 1],
                part_send.at[hop - 1], part_recv.at[hop - 1], device(plane, seat_to),
            )
        )
        parts[-1].start()
    held = [sent_ref[rows_of(seat)].astype(jnp.float32)]
    for hop in range(1, SIDE):
        parts[hop - 1].wait_recv()
        held.append(part_ref[hop - 1].astype(jnp.float32))
    total_ref[...] = functools.reduce(jnp.add, held).astype(jnp.bfloat16)
    planes = [
        copy(
            total_ref, plane_ref.at[hop - 1], plane_send.at[hop - 1], plane_recv.at[hop - 1],
            device((plane + hop) % SIDE, seat),
        )
        for hop in range(1, SIDE)
    ]
    for hop in range(1, SIDE):
        pl.when(plane + hop < SIDE)(planes[hop - 1].start)

    def earlier_seats(limit):
        total = jnp.zeros_like(held[0])
        for hop in range(SIDE):
            total = total + jnp.where((seat + SIDE - hop) % SIDE < limit, held[hop], 0.0)
        return total

    early_ref[...] = jnp.zeros_like(early_ref)
    for hop in range(1, SIDE):

        @pl.when(plane >= hop)
        def _(hop=hop):
            planes[hop - 1].wait_recv()
            early_ref[...] += plane_ref[hop - 1].astype(jnp.float32)

    early = early_ref[...]
    stages = []
    for hop in range(1, SIDE):
        seat_to = seat_after(hop)
        stage_ref[hop - 1] = early + earlier_seats(seat_to)
        stages.append(
            copy(
                stage_ref.at[hop - 1], before_ref.at[rows_of(seat)],
                stage_send.at[hop - 1], stage_recv.at[hop - 1], device(plane, seat_to),
            )
        )
        stages[-1].start()
    own_rows = rows_of(seat)

    def settle(rows, before):
        if last:
            out_ref[rows] = before + increment_ref[rows]
        else:
            out_ref[rows] = jnp.where(timestep == 0, latent_ref[rows], before)

    settle(own_rows, early + earlier_seats(seat))
    for hop in range(1, SIDE):
        stages[hop - 1].wait_recv()
        rows = rows_of((seat + SIDE - hop) % SIDE)
        settle(rows, before_ref[rows])
    for hop in range(1, SIDE):
        parts[hop - 1].wait_send()
        pl.when(plane + hop < SIDE)(planes[hop - 1].wait_send)
        stages[hop - 1].wait_send()


def carried_kernel(last, groups, sent, increment, latent):
    rows, lanes = sent.shape
    quarter = rows // SIDE
    hops = SIDE - 1
    vmem = pl.BlockSpec(memory_space=pltpu.VMEM)
    return pl.pallas_call(
        functools.partial(carry_kernel, last, groups),
        out_shape=jax.ShapeDtypeStruct((rows, lanes), jnp.float32),
        in_specs=[vmem] * 3,
        out_specs=vmem,
        scratch_shapes=[
            pltpu.VMEM((hops, quarter, lanes), jnp.bfloat16),
            pltpu.VMEM((quarter, lanes), jnp.bfloat16),
            pltpu.VMEM((hops, quarter, lanes), jnp.bfloat16),
            pltpu.VMEM((quarter, lanes), jnp.float32),
            pltpu.VMEM((hops, quarter, lanes), jnp.float32),
            pltpu.VMEM((rows, lanes), jnp.float32),
        ]
        + [pltpu.SemaphoreType.DMA((hops,))] * 6,
        compiler_params=pltpu.CompilerParams(collective_id=int(last), has_side_effects=True),
        name="carry_last" if last else "carry",
    )(sent, increment, latent)


def carried_in(last, groups, same_block, timestep, sent, increment, latent):
    rows = sent.size // LANES
    if sent.shape[-1] == LANES and rows % (SIDE * 16) == 0:
        flat = [array.reshape(rows, LANES) for array in (sent, increment, latent)]
        return carried_kernel(last, groups, *flat).reshape(latent.shape)
    gathered = lax.all_gather(
        sent, "tok", axis_index_groups=same_block if groups > 1 else None
    )
    earlier = (jnp.arange(P_SIZE) < timestep)[:, None, None, None]
    before = jnp.sum(jnp.where(earlier, gathered.astype(jnp.float32), 0.0), axis=0)
    return before + increment if last else jnp.where(timestep == 0, latent, before)


def body(
    initial_guess,
    noise_draws,
    drift_state,
    drift_denoise,
    noise_scale,
    modulation,
    embed_weight,
    space_input,
    space_output,
    time_input,
    time_output,
    final_weight,
):
    devices = lax.axis_size("tok")
    own_index = lax.axis_index("tok")
    groups = devices // P_SIZE
    timestep = own_index // groups
    own = jnp.reshape(timestep, (1,)).astype(jnp.int32)
    rates = (drift_state, drift_denoise, noise_scale)
    same_step = [[step * groups + block for block in range(groups)] for step in range(P_SIZE)]
    same_block = [[step * groups + block for step in range(P_SIZE)] for block in range(groups)]
    latent = initial_guess
    for iteration in range(ITERS):
        after = space_block(own, latent, modulation, embed_weight, space_input, space_output)
        if groups == 1:
            increment, sent = time_block(
                own, after, modulation, time_input, time_output, final_weight,
                (latent, noise_draws) + rates,
            )
        else:
            after = lax.all_to_all(
                after, "tok", split_axis=1, concat_axis=0, axis_index_groups=same_step, tiled=True
            )
            (predicted,) = time_block(own, after, modulation, time_input, time_output, final_weight)
            predicted = lax.all_to_all(
                predicted, "tok", split_axis=0, concat_axis=2, axis_index_groups=same_step, tiled=True
            )
            rate_state, rate_denoise, rate_noise = (
                lax.dynamic_index_in_dim(rate, timestep, 0, keepdims=False) for rate in rates
            )
            rate_state = rate_state + jnp.where(timestep == 0, 1.0, 0.0)
            increment = rate_state * latent + rate_denoise * predicted + rate_noise * noise_draws
            sent = increment.astype(jnp.bfloat16)
        latent = carried_in(
            iteration == ITERS - 1, groups, same_block, timestep, sent, increment, latent
        )
    return latent


def solution(mesh):
    placed = (
        P(("group", "tok"), None, None),
        P(("group", "tok"), None, None),
        P(),
        P(),
        P(),
        P(),
        P(),
        P(),
        P(),
        P(),
        P(),
        P(),
    )
    return jax.shard_map(
        body, mesh=mesh, in_specs=placed, out_specs=P(("group", "tok"), None, None), check_vma=False
    )
```

time: 357 us -> 242 us (0.68); the launches traced: 352 us -> 242 us
  waiting for transfers between devices: 74.2 us -> 0 us
  local copies, waits for them, and re-layouts: 58.1 us -> 25.5 us
  Pallas kernels: 192 us -> 216 us
  other arithmetic: 13.8 us -> 0 us
  between operations: 13.6 us -> 0.19 us
    all_gather x2 -> x0, waiting for transfers between devices: 74.1 us -> none  [body(): lax.all_gather(increment.astype(jnp.bfloat16), 'tok', axis_index_groups=s...]
    pallas_call x4 -> x6, Pallas kernels: 192 us -> 216 us  [the longest x2 98.5 us: time_block(): pl.pallas_call(functools.partial(time_kernel, bool(fused)), out_shape=[ja...]
    reshape x2 -> x0, local copies, waits for them, and re-layouts: 13.3 us -> none  [pad_input(): jnp.pad(parts, ((0, 0), (0, 0), (0, PADDED - INNER)))]
    pad x4 -> x0, local copies, waits for them, and re-layouts: 10.7 us -> none  [the longest x2 9.2 us: pad_input(): jnp.pad(parts, ((0, 0), (0, 0), (0, PADDED - INNER)))]
    select_n x3 -> x0, other arithmetic: 6.79 us -> none  [the longest x2 4.46 us: body(): increment = jnp.where(leading, increment + latent, increment)]
    unnamed x51 -> x46, local copies, waits for them, and re-layouts: 20 us -> 25.5 us
    select_n x3 -> x0, local copies, waits for them, and re-layouts: 4.84 us -> none  [the longest x2 2.65 us: body(): increment = jnp.where(leading, increment + latent, increment)]
    reduce_sum x2 -> x0, other arithmetic: 3.67 us -> none  [body(): jnp.sum(jnp.where(earlier, gathered.astype(jnp.float32), 0.0), axis=0)]
  transfers between devices with their start and end apart: 2 -> 0, of which waited for: 2 -> 0; matrix products, arithmetic and copies ran while one was open for 0% -> 0% of each run, Pallas kernels for 0% -> 0%
where the time goes in v2:
time: 242 us
  Pallas kernels  216 us (89%)
  local copies, waits for them, and re-layouts  25.5 us (11%)
    pallas_call x2, Pallas kernels, time_block(): pl.pallas_call(functools.partial(time_kernel, bool(fused)), out_shape=[ja...  98.5 us
    pallas_call x2, Pallas kernels, space_block(): pl.pallas_call(space_kernel, out_shape=jax.ShapeDtypeStruct((frames, spat...  90.2 us
    pallas_call x2, Pallas kernels, carried_kernel(): pl.pallas_call(functools.partial(carry_kernel, last, groups), out_shape=j...  27 us
    unnamed x46, local copies, waits for them, and re-layouts  25.5 us

profile of v2, /device:TPU:29, one launch (start us, length us, event | category | flops | bytes accessed | tf_op | source)
XLA Modules:
  0.0 241.5 jit_solution(5290341878247229485)
XLA Ops:
  0.0 1.0 copy.15.refs_5_
  1.0 6.4 %copy.13.input_ref = bf16[1152,1728]{1,0:T(8,128)(2,1)} copy(bf16[1152,1728]{0,1:T(8,128)(2,1)} %param.19) | data formatting | bytes 7962624 | tf_op args[7]
  7.4 0.0 copy-start.6
  7.4 0.0 copy-start.11
  7.4 0.0 copy-start.17
  7.4 6.6 %copy.14.refs_3_ = bf16[1152,1728]{1,0:T(8,128)(2,1)} copy(bf16[1152,1728]{0,1:T(8,128)(2,1)} %param.21) | data formatting | bytes 7962624 | tf_op args[9]
  14.0 0.0 copy-done.6
  14.0 0.0 copy-done.11
  14.0 0.0 copy-done.17
  14.0 0.0 copy-start.2
  14.0 2.2 copy-done.2
  16.2 0.0 copy-start.13
  16.2 1.1 copy-done.13
  17.3 0.0 copy-start
  17.3 0.0 copy-start.12
  17.3 0.0 copy-start.16
  17.3 0.0 copy-start.18
  17.3 0.0 copy-start.19
  17.3 0.0 copy-start.20
  17.3 45.1 %space_block.2.refs_1_ = bf16[16,128,1152]{2,1,0:T(8,128)(2,1)S(1)} custom-call(s32[1]{0:T(128)} %bitcast.step_ref.refs_0_, f32[16,16,128]{2,1,0:T(8,128)S(1)} %copy-done.6, f32[16,8,1152]{2,1,0:T(8,128)S(1)} %copy-done.13, bf16[16,1152]{1,0:T(8,128)(2,1)S(1)} %copy-done.17, bf16[1152,1728]{1,0:T(8,128)(2,1)S(1)} %copy-done.2, bf16[576,1152]{1,0:T(8,128)(2,1)S(1)} %copy-done.11), custom_call_target="tpu_custom_call" | custom-call | flops 13589544960 | bytes 16072704 | tf_op jit(solution)/shard_map/space_block/pallas_call | solution.py:220
  62.4 0.0 copy-done
  62.5 0.0 copy-done.12
  62.5 0.0 copy-done.14
  62.5 0.0 copy-done.16
  62.5 0.0 copy-done.18
  62.5 0.0 copy-done.19
  62.5 0.0 copy-done.20
  62.5 49.3 %time_block.2 = (f32[16,16,128]{2,1,0:T(8,128)S(1)}, bf16[16,16,128]{2,1,0:T(8,128)(2,1)S(1)}) custom-call(s32[1]{0:T(128)} %bitcast.step_ref.refs_0_, bf16[16,128,1152]{2,1,0:T(8,128)(2,1)S(1)} %space_block.2.refs_1_, f32[16,8,1152]{2,1,0:T(8,128)S(1)} %copy-done.14, bf16[1152,1728]{1,0:T(8,128)(2,1)S(1)} %copy-done, bf16[576,1152]{1,0:T(8,128)(2,1)S(1)} %copy-done.12, ...), custom_call_target="tpu_custom_call" | custom-call | flops 13589544960 | bytes 16072704 | tf_op jit(solution)/shard_map/time_block/pallas_call | solution.py:253
  111.8 0.0 copy-start.8
  111.8 0.6 copy-done.8
  112.4 0.0 copy-start.10
  112.4 0.6 copy-done.10
  113.1 13.7 %carry.1.latent_ref = f32[256,128]{1,0:T(8,128)} custom-call(bf16[256,128]{1,0:T(8,128)(2,1)} %bitcast.14, f32[256,128]{1,0:T(8,128)} %bitcast.12, f32[256,128]{1,0:T(8,128)} %bitcast.10), custom_call_target="tpu_custom_call" | custom-call | tf_op jit(solution)/shard_map/carry/pallas_call | solution.py:399
  126.8 0.0 copy-start.3
  126.8 2.2 copy-done.3
  128.9 0.0 copy-start.4
  128.9 0.9 copy-done.4
  129.8 1.1 copy-done.15
  130.9 0.0 copy-start.1
  130.9 45.1 %space_block.3.refs_1_ = bf16[16,128,1152]{2,1,0:T(8,128)(2,1)S(1)} custom-call(s32[1]{0:T(128)} %bitcast.step_ref.refs_0_, f32[16,16,128]{2,1,0:T(8,128)S(1)} %bitcast.8, f32[16,8,1152]{2,1,0:T(8,128)S(1)} %copy-done.15, bf16[16,1152]{1,0:T(8,128)(2,1)S(1)} %copy-done.17, bf16[1152,1728]{1,0:T(8,128)(2,1)S(1)} %copy-done.3, bf16[576,1152]{1,0:T(8,128)(2,1)S(1)} %copy-done.11), custom_call_target="tpu_custom_call" | custom-call | flops 13589544960 | bytes 16072704 | tf_op jit(solution)/shard_map/space_block/pallas_call | solution.py:220
  176.0 0.0 copy-done.1
  176.0 0.0 copy-done.5
  176.0 49.3 %time_block.3 = (f32[16,16,128]{2,1,0:T(8,128)S(1)}, bf16[16,16,128]{2,1,0:T(8,128)(2,1)S(1)}) custom-call(s32[1]{0:T(128)} %bitcast.step_ref.refs_0_, bf16[16,128,1152]{2,1,0:T(8,128)(2,1)S(1)} %space_block.3.refs_1_, f32[16,8,1152]{2,1,0:T(8,128)S(1)} %copy-done.15, bf16[1152,1728]{1,0:T(8,128)(2,1)S(1)} %copy-done.1, bf16[576,1152]{1,0:T(8,128)(2,1)S(1)} %copy-done.12, ...), custom_call_target="tpu_custom_call" | custom-call | flops 13589544960 | bytes 16072704 | tf_op jit(solution)/shard_map/time_block/pallas_call | solution.py:253
  225.3 0.0 copy-start.7
  225.3 0.6 copy-done.7
  226.0 0.6 copy-done.9
  226.6 13.3 %carry_last.1 = f32[256,128]{1,0:T(8,128)} custom-call(bf16[256,128]{1,0:T(8,128)(2,1)} %bitcast.13, f32[256,128]{1,0:T(8,128)} %bitcast.11, f32[256,128]{1,0:T(8,128)} %carry.1.latent_ref), custom_call_target="tpu_custom_call" | custom-call | tf_op jit(solution)/shard_map/carry_last/pallas_call | solution.py:399
  239.9 1.6 copy.20
  (4 shorter events, 0.0 us)
Async XLA Ops:
  7.4 6.6 %copy-start.6 = (f32[16,16,128]{2,1,0:T(8,128)S(1)}, f32[16,16,128]{2,1,0:T(8,128)}, u32[]{:S(2)}) copy-start(f32[16,16,128]{2,1,0:T(8,128)} %refs_6_.1) | copy-start | bytes 393220
  7.4 6.6 %copy-start.11 = (bf16[576,1152]{1,0:T(8,128)(2,1)S(1)}, bf16[576,1152]{1,0:T(8,128)(2,1)}, u32[]{:S(2)}) copy-start(bf16[576,1152]{1,0:T(8,128)(2,1)} %output_ref.3) | copy-start | bytes 3981316
  7.4 6.6 %copy-start.17 = (bf16[16,1152]{1,0:T(8,128)(2,1)S(1)}, bf16[16,1152]{1,0:T(8,128)(2,1)}, u32[]{:S(2)}) copy-start(bf16[16,1152]{1,0:T(8,128)(2,1)} %embed_ref.3) | copy-start | bytes 110596
  14.0 2.2 copy-start.2
  16.2 1.1 copy-start.13
  17.3 45.2 %copy-start = (bf16[1152,1728]{1,0:T(8,128)(2,1)S(1)}, bf16[1152,1728]{1,0:T(8,128)(2,1)}, u32[]{:S(2)}) copy-start(bf16[1152,1728]{1,0:T(8,128)(2,1)} %copy.14.refs_3_) | copy-start | bytes 11943940
  17.3 45.2 %copy-start.12 = (bf16[576,1152]{1,0:T(8,128)(2,1)S(1)}, bf16[576,1152]{1,0:T(8,128)(2,1)}, u32[]{:S(2)}) copy-start(bf16[576,1152]{1,0:T(8,128)(2,1)} %refs_4_.3) | copy-start | bytes 3981316
  17.3 45.2 %copy-start.14 = (f32[16,8,1152]{2,1,0:T(8,128)S(1)}, f32[16,8,1152]{2,1,0:T(8,128)}, u32[]{:S(2)}) copy-start(f32[16,8,1152]{2,1,0:T(8,128)} %refs_2_.3) | copy-start | bytes 1769476
  17.3 45.2 %copy-start.16 = (f32[16,16,128]{2,1,0:T(8,128)S(1)}, f32[16,16,128]{2,1,0:T(8,128)}, u32[]{:S(2)}) copy-start(f32[16,16,128]{2,1,0:T(8,128)} %refs_7_.3) | copy-start | bytes 393220
  17.3 45.2 %copy-start.18 = (f32[16]{0:T(128)S(1)}, f32[16]{0:T(128)}, u32[]{:S(2)}) copy-start(f32[16]{0:T(128)} %refs_8_.3) | copy-start | bytes 196
  17.3 45.2 %copy-start.19 = (f32[16]{0:T(128)S(1)}, f32[16]{0:T(128)}, u32[]{:S(2)}) copy-start(f32[16]{0:T(128)} %refs_9_.3) | copy-start | bytes 196
  17.3 45.2 %copy-start.20 = (f32[16]{0:T(128)S(1)}, f32[16]{0:T(128)}, u32[]{:S(2)}) copy-start(f32[16]{0:T(128)} %refs_10_.3) | copy-start | bytes 196
  111.8 0.7 copy-start.8
  112.4 0.6 copy-start.10
  126.8 2.2 copy-start.3
  128.9 0.9 copy-start.4
  129.8 1.1 copy-start.15
  130.9 45.1 %copy-start.1 = (bf16[1152,1728]{1,0:T(8,128)(2,1)S(1)}, bf16[1152,1728]{1,0:T(8,128)(2,1)}, u32[]{:S(2)}) copy-start(bf16[1152,1728]{1,0:T(8,128)(2,1)} %copy.14.refs_3_) | copy-start | bytes 11943940
  130.9 45.1 %copy-start.5 = (f32[256,128]{1,0:T(8,128)S(1)}, f32[256,128]{1,0:T(8,128)}, u32[]{:S(2)}) copy-start(f32[256,128]{1,0:T(8,128)} %carry.1.latent_ref) | copy-start | bytes 393220
  225.3 0.7 copy-start.7
  226.0 0.6 copy-start.9

commit v3 on v2

--- a/solution.py
+++ b/solution.py
@@ -24,6 +24,12 @@
     return center * lax.rsqrt(jnp.mean(center * center, -1, keepdims=True) + 1e-06)
 
 
+def dot_rows(values, weight_rows):
+    return lax.dot_general(
+        values, weight_rows, (((1,), (1,)), ((), ())), preferred_element_type=jnp.float32
+    )
+
+
 def head_slab(head):
     first = head * HD // LANES
     last = (head * HD + HD - 1) // LANES
@@ -42,43 +48,56 @@
     return pltpu.roll(packed[:, low : low + PADDED], PADDED - (INNER - low), 1)
 
 
-def attend(read, write, rows, keep):
+def attend(blocks, rows, keep):
     lane = lax.broadcasted_iota(jnp.int32, (rows, LANES), 1)
-    outs = []
-    for head in range(HEADS):
+    open_tiles = {}
+    units = [(head, place) for head in range(HEADS) for place in range(len(blocks))]
+
+    def prepare(unit):
+        head, place = unit
+        read = blocks[place][0]
         tile, tiles = head_slab(head)
         low = head * HD - tile * LANES
-        width = tiles * LANES
-        lanes = lax.broadcasted_iota(jnp.int32, (rows, width), 1)
+        lanes = lax.broadcasted_iota(jnp.int32, (rows, tiles * LANES), 1)
         inside = (lanes >= low) & (lanes < low + HD)
         queries = jnp.where(inside, read(0, tile, tiles), 0.0)
         keys = jnp.where(inside, read(1, tile, tiles), 0.0)
-        values = read(2, tile, tiles).astype(jnp.bfloat16)
         query_rate = lax.rsqrt(jnp.sum(queries * queries, -1, keepdims=True) / HD + 1e-06)
         key_rate = lax.rsqrt(jnp.sum(keys * keys, -1, keepdims=True) / HD + 1e-06)
         queries = (queries * (query_rate * (HD**-0.5 * math.log2(math.e)))).astype(jnp.bfloat16)
-        keys = (keys * key_rate).astype(jnp.bfloat16)
-        scores = lax.dot_general(
-            queries, keys, (((1,), (1,)), ((), ())), preferred_element_type=jnp.float32
-        )
-        weights = jnp.exp2(scores)
+        return queries, (keys * key_rate).astype(jnp.bfloat16)
+
+    def weigh(unit, prepared):
+        weights = jnp.exp2(dot_rows(*prepared))
         if keep is not None:
             weights = jnp.where(keep, weights, 0.0)
-        weights = weights * (1.0 / jnp.sum(weights, -1, keepdims=True))
-        outs.append(
-            jnp.dot(weights.astype(jnp.bfloat16), values, preferred_element_type=jnp.float32)
-        )
-    for tile in range(PADDED // LANES):
-        total = None
-        for head in range(HEADS):
-            first, tiles = head_slab(head)
-            if first <= tile < first + tiles:
-                part = outs[head][:, (tile - first) * LANES : (tile - first + 1) * LANES]
-                if total is None:
-                    total = part
-                else:
-                    total = jnp.where(lane >= head * HD - tile * LANES, part, total)
-        write(tile, total)
+        return (weights * (1.0 / jnp.sum(weights, -1, keepdims=True))).astype(jnp.bfloat16)
+
+    def mix(unit, weights):
+        head, place = unit
+        read, write = blocks[place]
+        tile, tiles = head_slab(head)
+        values = read(2, tile, tiles).astype(jnp.bfloat16)
+        mixed = jnp.dot(weights, values, preferred_element_type=jnp.float32)
+        for own in range(tile, tile + tiles):
+            part = mixed[:, (own - tile) * LANES : (own - tile + 1) * LANES]
+            if (place, own) in open_tiles:
+                part = jnp.where(
+                    lane >= head * HD - own * LANES, part, open_tiles.pop((place, own))
+                )
+            if (head + 1) * HD >= min((own + 1) * LANES, INNER):
+                write(own, part)
+            else:
+                open_tiles[place, own] = part
+
+    prepared, weighed = {}, {}
+    for at in range(len(units) + 8):
+        if at < len(units):
+            prepared[at] = prepare(units[at])
+        if 0 <= at - 4 < len(units):
+            weighed[at - 4] = weigh(units[at - 4], prepared.pop(at - 4))
+        if 0 <= at - 8 < len(units):
+            mix(units[at - 8], weighed.pop(at - 8))
 
 
 def space_kernel(
@@ -96,12 +115,12 @@
     normed = (
         layer_norm(embedded_ref[...]) * (1.0 + table_ref[1:2, :]) + table_ref[0:1, :]
     ).astype(jnp.bfloat16)
-    packed = jnp.dot(normed, input_ref[...], preferred_element_type=jnp.float32)
+    packed = dot_rows(normed, input_ref[...])
     packed_ref[...] = packed
     key_ref[...] = lined_keys(packed)
 
-    def one(frame, carry):
-        rows = pl.ds(pl.multiple_of(frame * spatial, spatial), spatial)
+    def one(frame):
+        rows = slice(frame * spatial, (frame + 1) * spatial)
 
         def read(part, tile, tiles):
             source, start, stop = part_lanes(part, tile, tiles)
@@ -110,10 +129,9 @@
         def write(tile, values):
             mixed_ref[rows, tile * LANES : tile * LANES + values.shape[1]] = values
 
-        attend(read, write, spatial, None)
-        return carry
-
-    lax.fori_loop(0, frames, one, 0)
+        return read, write
+
+    attend([one(frame) for frame in range(frames)], spatial, None)
     result = jnp.dot(
         mixed_ref[...].astype(jnp.bfloat16), output_ref[...], preferred_element_type=jnp.float32
     )
@@ -136,15 +154,15 @@
     normed = (layer_norm(hidden) * (1.0 + table_ref[4:5, :]) + table_ref[3:4, :]).astype(
         jnp.bfloat16
     )
-    packed = jnp.dot(normed, input_ref[...], preferred_element_type=jnp.float32)
+    packed = dot_rows(normed, input_ref[...])
     packed_ref[...] = packed.reshape(packed_ref.shape)
     key_ref[...] = lined_keys(packed).reshape(key_ref.shape)
     keep = (lax.broadcasted_iota(jnp.int32, (rows, rows), 0) % chunk) == (
         lax.broadcasted_iota(jnp.int32, (rows, rows), 1) % chunk
     )
 
-    def one(index, carry):
-        own = pl.ds(pl.multiple_of(index * chunk, chunk), chunk)
+    def one(index):
+        own = slice(index * chunk, (index + 1) * chunk)
 
         def read(part, tile, tiles):
             source, start, stop = part_lanes(part, tile, tiles)
@@ -156,10 +174,9 @@
                 frames, chunk, lanes
             )
 
-        attend(read, write, rows, keep)
-        return carry
-
-    lax.fori_loop(0, positions // chunk, one, 0)
+        return read, write
+
+    attend([one(index) for index in range(positions // chunk)], rows, keep)
     mixed = mixed_ref[...].reshape(tokens, INNER).astype(jnp.bfloat16)
     result = jnp.dot(mixed, output_ref[...], preferred_element_type=jnp.float32)
     hidden = after_ref[...].reshape(tokens, width).astype(jnp.float32)
@@ -167,7 +184,7 @@
     normed = (layer_norm(settled) * (1.0 + table_ref[7:8, :]) + table_ref[6:7, :]).astype(
         jnp.bfloat16
     )
-    predicted = jnp.dot(normed, final_ref[...], preferred_element_type=jnp.float32)
+    predicted = dot_rows(normed, final_ref[...])
     own = pl.ds(pl.multiple_of(pl.program_id(0) * positions, positions), positions)
     predicted_ref[:, own, :] = predicted.reshape(frames, positions, predicted.shape[1])
 
@@ -207,7 +224,7 @@
 def cost_of(tokens, *weights):
     return pl.CostEstimate(
         flops=2 * tokens * sum(weight.size for weight in weights),
-        bytes_accessed=2 * sum(weight.size for weight in weights) + 4 * tokens * weights[0].shape[0],
+        bytes_accessed=2 * sum(weight.size for weight in weights) + 4 * tokens * weights[0].shape[-1],
         transcendentals=0,
     )
 
@@ -246,7 +263,7 @@
 
 def time_block(own, after, modulation, input_weight, output_weight, final_weight, fused=()):
     frames, positions, width = after.shape
-    channels = final_weight.shape[1]
+    channels = final_weight.shape[0]
     step_positions = math.gcd(positions, max(16, BLOCK_TOKENS // frames))
     shape = (frames, channels, positions)
     kinds = [jnp.float32] + [jnp.bfloat16] * bool(fused)
@@ -450,6 +467,7 @@
     rates = (drift_state, drift_denoise, noise_scale)
     same_step = [[step * groups + block for block in range(groups)] for step in range(P_SIZE)]
     same_block = [[step * groups + block for step in range(P_SIZE)] for block in range(groups)]
+    space_input, time_input, final_weight = space_input.T, time_input.T, final_weight.T
     latent = initial_guess
     for iteration in range(ITERS):
         after = space_block(own, latent, modulation, embed_weight, space_input, space_output)

time: 242 us -> 169 us (0.70)
  Pallas kernels: 216 us -> 154 us
  local copies, waits for them, and re-layouts: 25.5 us -> 13.4 us
    pallas_call x2, Pallas kernels: 90.2 us -> 58 us  [space_block(): pl.pallas_call(space_kernel, out_shape=jax.ShapeDtypeStruct((frames, spat...]
    pallas_call x2, Pallas kernels: 98.5 us -> 69.4 us  [time_block(): pl.pallas_call(functools.partial(time_kernel, bool(fused)), out_shape=[ja...]
    unnamed x46 -> x49, local copies, waits for them, and re-layouts: 25.5 us -> 13.4 us
where the time goes in v3:
time: 169 us; the launch traced here: 168 us
  Pallas kernels  154 us (91%)
  local copies, waits for them, and re-layouts  13.4 us (8%)
    pallas_call x2, Pallas kernels, time_block(): pl.pallas_call(functools.partial(time_kernel, bool(fused)), out_shape=[ja...  69.4 us
    pallas_call x2, Pallas kernels, space_block(): pl.pallas_call(space_kernel, out_shape=jax.ShapeDtypeStruct((frames, spat...  58 us
    pallas_call x2, Pallas kernels, carried_kernel(): pl.pallas_call(functools.partial(carry_kernel, last, groups), out_shape=j...  27.1 us
    unnamed x49, local copies, waits for them, and re-layouts  13.4 us

profile of v3, /device:TPU:29, one launch (start us, length us, event | category | flops | bytes accessed | tf_op | source)
XLA Modules:
  0.0 168.1 jit_solution(18294406943860553722)
XLA Ops:
  0.0 0.0 copy-start.2
  0.0 0.9 copy-done.2
  0.9 0.0 copy-start.7
  0.9 2.1 %copy-done.7 = bf16[1152,1728]{0,1:T(8,128)(2,1)S(1)} copy-done((bf16[1152,1728]{0,1:T(8,128)(2,1)S(1)}, bf16[1152,1728]{0,1:T(8,128)(2,1)}, u32[]{:S(2)}) %copy-start.7) | copy-done | bytes 3981336
  3.0 0.0 copy-start.11
  3.0 1.3 copy-done.11
  4.4 0.0 copy-start.14
  4.4 1.1 copy-done.14
  5.4 0.0 copy-start.17
  5.4 0.8 copy-done.17
  6.2 0.0 copy-start.9
  6.2 0.0 copy-start.13
  6.2 0.0 copy-start.16
  6.2 0.0 copy-start.21
  6.2 0.0 copy-start.22
  6.2 0.0 copy-start.23
  6.2 29.0 %space_block.2.refs_1_ = bf16[16,128,1152]{2,1,0:T(8,128)(2,1)S(1)} custom-call(s32[1]{0:T(128)} %bitcast.step_ref.refs_0_, f32[16,16,128]{2,1,0:T(8,128)S(1)} %copy-done.2, f32[16,8,1152]{2,1,0:T(8,128)S(1)} %copy-done.14, bf16[16,1152]{1,0:T(8,128)(2,1)S(1)} %copy-done.17, bf16[1728,1152]{1,0:T(8,128)(2,1)S(1)} %bitcast.18, bf16[576,1152]{1,0:T(8,128)(2,1)S(1)} %copy-done.11), custom_call_target="tpu_custom_call" | custom-call | flops 13589544960 | bytes 16072704 | tf_op jit(solution)/shard_map/space_block/pallas_call | solution.py:237
  35.3 0.0 copy-done.9
  35.3 0.0 copy-done.13
  35.3 0.0 copy-done.16
  35.3 0.0 copy-done.19
  35.3 0.0 copy-done.21
  35.3 0.0 copy-done.22
  35.3 0.0 copy-done.23
  35.4 0.0 copy-start.12
  35.4 0.0 copy-start.15
  35.4 0.0 copy-start.18
  35.4 34.7 %time_block.2 = (f32[16,16,128]{2,1,0:T(8,128)S(1)}, bf16[16,16,128]{2,1,0:T(8,128)(2,1)S(1)}) custom-call(s32[1]{0:T(128)} %bitcast.step_ref.refs_0_, bf16[16,128,1152]{2,1,0:T(8,128)(2,1)S(1)} %space_block.2.refs_1_, f32[16,8,1152]{2,1,0:T(8,128)S(1)} %copy-done.14, bf16[1728,1152]{1,0:T(8,128)(2,1)S(1)} %bitcast.20, bf16[576,1152]{1,0:T(8,128)(2,1)S(1)} %copy-done.13, ...), custom_call_target="tpu_custom_call" | custom-call | flops 13589544960 | bytes 16072704 | tf_op jit(solution)/shard_map/time_block/pallas_call | solution.py:270
  70.1 0.0 copy-start.4
  70.1 0.6 copy-done.4
  70.8 0.6 copy-done.6
  71.4 13.8 %carry.1.latent_ref = f32[256,128]{1,0:T(8,128)} custom-call(bf16[256,128]{1,0:T(8,128)(2,1)} %bitcast.17, f32[256,128]{1,0:T(8,128)} %bitcast.15, f32[256,128]{1,0:T(8,128)} %bitcast.13), custom_call_target="tpu_custom_call" | custom-call | tf_op jit(solution)/shard_map/carry/pallas_call | solution.py:416
  85.1 0.0 copy-done.12
  85.2 0.0 copy-done.15
  85.2 0.0 copy-done.18
  85.2 0.0 copy-start
  85.2 0.9 copy-done
  86.1 2.1 %copy-done.8 = bf16[1152,1728]{0,1:T(8,128)(2,1)S(1)} copy-done((bf16[1152,1728]{0,1:T(8,128)(2,1)S(1)}, bf16[1152,1728]{0,1:T(8,128)(2,1)}, u32[]{:S(2)}) %copy-start.8) | copy-done | bytes 3981336
  88.2 28.9 %space_block.3.refs_1_ = bf16[16,128,1152]{2,1,0:T(8,128)(2,1)S(1)} custom-call(s32[1]{0:T(128)} %bitcast.step_ref.refs_0_, f32[16,16,128]{2,1,0:T(8,128)S(1)} %bitcast.11, f32[16,8,1152]{2,1,0:T(8,128)S(1)} %copy-done.15, bf16[16,1152]{1,0:T(8,128)(2,1)S(1)} %copy-done.18, bf16[1728,1152]{1,0:T(8,128)(2,1)S(1)} %bitcast.19, bf16[576,1152]{1,0:T(8,128)(2,1)S(1)} %copy-done.12), custom_call_target="tpu_custom_call" | custom-call | flops 13589544960 | bytes 16072704 | tf_op jit(solution)/shard_map/space_block/pallas_call | solution.py:237
  117.1 0.0 copy-done.1
  117.1 0.0 copy-done.10
  117.2 0.0 copy-done.20
  117.2 34.7 %time_block.3 = (f32[16,16,128]{2,1,0:T(8,128)S(1)}, bf16[16,16,128]{2,1,0:T(8,128)(2,1)S(1)}) custom-call(s32[1]{0:T(128)} %bitcast.step_ref.refs_0_, bf16[16,128,1152]{2,1,0:T(8,128)(2,1)S(1)} %space_block.3.refs_1_, f32[16,8,1152]{2,1,0:T(8,128)S(1)} %copy-done.15, bf16[1728,1152]{1,0:T(8,128)(2,1)S(1)} %bitcast.21, bf16[576,1152]{1,0:T(8,128)(2,1)S(1)} %copy-done.13, ...), custom_call_target="tpu_custom_call" | custom-call | flops 13589544960 | bytes 16072704 | tf_op jit(solution)/shard_map/time_block/pallas_call | solution.py:270
  151.9 0.0 copy-start.3
  151.9 0.6 copy-done.3
  152.5 0.6 copy-done.5
  153.2 13.3 %carry_last.1 = f32[256,128]{1,0:T(8,128)} custom-call(bf16[256,128]{1,0:T(8,128)(2,1)} %bitcast.16, f32[256,128]{1,0:T(8,128)} %bitcast.14, f32[256,128]{1,0:T(8,128)} %carry.1.latent_ref), custom_call_target="tpu_custom_call" | custom-call | tf_op jit(solution)/shard_map/carry_last/pallas_call | solution.py:416
  166.5 1.6 copy.14
  (7 shorter events, 0.0 us)
Async XLA Ops:
  0.0 0.9 copy-start.2
  0.9 2.1 %copy-start.7 = (bf16[1152,1728]{0,1:T(8,128)(2,1)S(1)}, bf16[1152,1728]{0,1:T(8,128)(2,1)}, u32[]{:S(2)}) copy-start(bf16[1152,1728]{0,1:T(8,128)(2,1)} %param.19) | copy-start | bytes 11943940
  3.0 1.3 copy-start.11
  4.4 1.1 copy-start.14
  5.4 0.8 copy-start.17
  6.2 29.1 %copy-start.9 = (bf16[1152,1728]{0,1:T(8,128)(2,1)S(1)}, bf16[1152,1728]{0,1:T(8,128)(2,1)}, u32[]{:S(2)}) copy-start(bf16[1152,1728]{0,1:T(8,128)(2,1)} %param.21) | copy-start | bytes 11943940
  6.2 29.1 %copy-start.13 = (bf16[576,1152]{1,0:T(8,128)(2,1)S(1)}, bf16[576,1152]{1,0:T(8,128)(2,1)}, u32[]{:S(2)}) copy-start(bf16[576,1152]{1,0:T(8,128)(2,1)} %refs_4_.3) | copy-start | bytes 3981316
  6.2 29.1 %copy-start.16 = (f32[16,16,128]{2,1,0:T(8,128)S(1)}, f32[16,16,128]{2,1,0:T(8,128)}, u32[]{:S(2)}) copy-start(f32[16,16,128]{2,1,0:T(8,128)} %refs_7_.3) | copy-start | bytes 393220
  6.2 29.1 %copy-start.19 = (bf16[1152,16]{0,1:T(8,128)(2,1)S(1)}, bf16[1152,16]{0,1:T(8,128)(2,1)}, u32[]{:S(2)}) copy-start(bf16[1152,16]{0,1:T(8,128)(2,1)} %param.23) | copy-start | bytes 110596
  6.2 29.1 %copy-start.21 = (f32[16]{0:T(128)S(1)}, f32[16]{0:T(128)}, u32[]{:S(2)}) copy-start(f32[16]{0:T(128)} %refs_8_.3) | copy-start | bytes 196
  6.2 29.1 %copy-start.22 = (f32[16]{0:T(128)S(1)}, f32[16]{0:T(128)}, u32[]{:S(2)}) copy-start(f32[16]{0:T(128)} %refs_9_.3) | copy-start | bytes 196
  6.2 29.1 %copy-start.23 = (f32[16]{0:T(128)S(1)}, f32[16]{0:T(128)}, u32[]{:S(2)}) copy-start(f32[16]{0:T(128)} %refs_10_.3) | copy-start | bytes 196
  35.4 49.8 %copy-start.12 = (bf16[576,1152]{1,0:T(8,128)(2,1)S(1)}, bf16[576,1152]{1,0:T(8,128)(2,1)}, u32[]{:S(2)}) copy-start(bf16[576,1152]{1,0:T(8,128)(2,1)} %output_ref.3) | copy-start | bytes 3981316
  35.4 49.8 %copy-start.15 = (f32[16,8,1152]{2,1,0:T(8,128)S(1)}, f32[16,8,1152]{2,1,0:T(8,128)}, u32[]{:S(2)}) copy-start(f32[16,8,1152]{2,1,0:T(8,128)} %refs_2_.3) | copy-start | bytes 1769476
  35.4 49.8 %copy-start.18 = (bf16[16,1152]{1,0:T(8,128)(2,1)S(1)}, bf16[16,1152]{1,0:T(8,128)(2,1)}, u32[]{:S(2)}) copy-start(bf16[16,1152]{1,0:T(8,128)(2,1)} %embed_ref.3) | copy-start | bytes 110596
  70.1 0.7 copy-start.4
  70.8 0.6 copy-start.6
  85.2 0.9 copy-start
  86.1 2.1 %copy-start.8 = (bf16[1152,1728]{0,1:T(8,128)(2,1)S(1)}, bf16[1152,1728]{0,1:T(8,128)(2,1)}, u32[]{:S(2)}) copy-start(bf16[1152,1728]{0,1:T(8,128)(2,1)} %param.19) | copy-start | bytes 11943940
  88.2 28.9 %copy-start.1 = (f32[256,128]{1,0:T(8,128)S(1)}, f32[256,128]{1,0:T(8,128)}, u32[]{:S(2)}) copy-start(f32[256,128]{1,0:T(8,128)} %carry.1.latent_ref) | copy-start | bytes 393220
  88.2 28.9 %copy-start.10 = (bf16[1152,1728]{0,1:T(8,128)(2,1)S(1)}, bf16[1152,1728]{0,1:T(8,128)(2,1)}, u32[]{:S(2)}) copy-start(bf16[1152,1728]{0,1:T(8,128)(2,1)} %param.21) | copy-start | bytes 11943940
  88.2 28.9 %copy-start.20 = (bf16[1152,16]{0,1:T(8,128)(2,1)S(1)}, bf16[1152,16]{0,1:T(8,128)(2,1)}, u32[]{:S(2)}) copy-start(bf16[1152,16]{0,1:T(8,128)(2,1)} %param.23) | copy-start | bytes 110596
  151.9 0.7 copy-start.3
  152.5 0.6 copy-start.5

commit v4 on v3

--- a/solution.py
+++ b/solution.py
@@ -48,7 +48,7 @@
     return pltpu.roll(packed[:, low : low + PADDED], PADDED - (INNER - low), 1)
 
 
-def attend(blocks, rows, keep):
+def attend(blocks, rows, keep, lags):
     lane = lax.broadcasted_iota(jnp.int32, (rows, LANES), 1)
     open_tiles = {}
     units = [(head, place) for head in range(HEADS) for place in range(len(blocks))]
@@ -71,16 +71,24 @@
         weights = jnp.exp2(dot_rows(*prepared))
         if keep is not None:
             weights = jnp.where(keep, weights, 0.0)
-        return (weights * (1.0 / jnp.sum(weights, -1, keepdims=True))).astype(jnp.bfloat16)
+        return weights.astype(jnp.bfloat16)
 
     def mix(unit, weights):
         head, place = unit
         read, write = blocks[place]
         tile, tiles = head_slab(head)
         values = read(2, tile, tiles).astype(jnp.bfloat16)
+        ones = jnp.ones((rows, LANES), jnp.bfloat16)
+        if tiles == 1:
+            values = jnp.concatenate([values, ones], axis=1)
         mixed = jnp.dot(weights, values, preferred_element_type=jnp.float32)
+        total = mixed[:, LANES:] if tiles == 1 else jnp.dot(
+            weights, ones, preferred_element_type=jnp.float32
+        )
+        share = 1.0 / total
         for own in range(tile, tile + tiles):
-            part = mixed[:, (own - tile) * LANES : (own - tile + 1) * LANES]
+            part = mixed[:, (own - tile) * LANES : min((own - tile + 1) * LANES, values.shape[1])]
+            part = part * share[:, : part.shape[1]]
             if (place, own) in open_tiles:
                 part = jnp.where(
                     lane >= head * HD - own * LANES, part, open_tiles.pop((place, own))
@@ -91,13 +99,13 @@
                 open_tiles[place, own] = part
 
     prepared, weighed = {}, {}
-    for at in range(len(units) + 8):
+    for at in range(len(units) + lags[1]):
         if at < len(units):
             prepared[at] = prepare(units[at])
-        if 0 <= at - 4 < len(units):
-            weighed[at - 4] = weigh(units[at - 4], prepared.pop(at - 4))
-        if 0 <= at - 8 < len(units):
-            mix(units[at - 8], weighed.pop(at - 8))
+        if 0 <= at - lags[0] < len(units):
+            weighed[at - lags[0]] = weigh(units[at - lags[0]], prepared.pop(at - lags[0]))
+        if 0 <= at - lags[1] < len(units):
+            mix(units[at - lags[1]], weighed.pop(at - lags[1]))
 
 
 def space_kernel(
@@ -131,7 +139,7 @@
 
         return read, write
 
-    attend([one(frame) for frame in range(frames)], spatial, None)
+    attend([one(frame) for frame in range(frames)], spatial, None, (3, 6))
     result = jnp.dot(
         mixed_ref[...].astype(jnp.bfloat16), output_ref[...], preferred_element_type=jnp.float32
     )
@@ -176,7 +184,7 @@
 
         return read, write
 
-    attend([one(index) for index in range(positions // chunk)], rows, keep)
+    attend([one(index) for index in range(positions // chunk)], rows, keep, (4, 8))
     mixed = mixed_ref[...].reshape(tokens, INNER).astype(jnp.bfloat16)
     result = jnp.dot(mixed, output_ref[...], preferred_element_type=jnp.float32)
     hidden = after_ref[...].reshape(tokens, width).astype(jnp.float32)
@@ -255,7 +263,7 @@
                 pltpu.VMEM((tokens, INNER), jnp.float32),
             ],
         ),
-        compiler_params=pltpu.CompilerParams(vmem_limit_bytes=36 * 1024 * 1024),
+        compiler_params=pltpu.CompilerParams(vmem_limit_bytes=60 * 1024 * 1024),
         cost_estimate=cost_of(frames * spatial, input_weight, output_weight, output_weight),
         name="space_block",
     )(own, latent, modulation, embed_weight, input_weight, output_weight)
@@ -295,7 +303,7 @@
                 pltpu.VMEM((frames, step_positions, INNER), jnp.float32),
             ],
         ),
-        compiler_params=pltpu.CompilerParams(vmem_limit_bytes=36 * 1024 * 1024),
+        compiler_params=pltpu.CompilerParams(vmem_limit_bytes=60 * 1024 * 1024),
         cost_estimate=cost_of(frames * positions, input_weight, output_weight, output_weight),
         name="time_block",
     )(own, after, modulation, input_weight, output_weight, final_weight, *fused)

time: 169 us -> 157 us (0.929)
  local copies, waits for them, and re-layouts: 13.4 us -> 1.57 us
    unnamed x49 -> x1, local copies, waits for them, and re-layouts: 13.4 us -> 1.57 us
where the time goes in v4:
time: 157 us
  Pallas kernels  155 us (99%)
  local copies, waits for them, and re-layouts  1.57 us (1%)
    pallas_call x2, Pallas kernels, time_block(): pl.pallas_call(functools.partial(time_kernel, bool(fused)), out_shape=[ja...  70 us
    pallas_call x2, Pallas kernels, space_block(): pl.pallas_call(space_kernel, out_shape=jax.ShapeDtypeStruct((frames, spat...  58.2 us
    pallas_call x2, Pallas kernels, carried_kernel(): pl.pallas_call(functools.partial(carry_kernel, last, groups), out_shape=j...  27.1 us

profile of v4, /device:TPU:29, one launch (start us, length us, event | category | flops | bytes accessed | tf_op | source)
XLA Modules:
  0.0 156.8 jit_solution(6933351060187633769)
XLA Ops:
  0.0 29.1 %space_block.2.refs_1_ = bf16[16,128,1152]{2,1,0:T(8,128)(2,1)} custom-call(s32[1]{0:T(128)} %bitcast.step_ref.refs_0_, f32[16,16,128]{2,1,0:T(8,128)} %refs_6_.1, f32[16,8,1152]{2,1,0:T(8,128)} %refs_2_.3, bf16[16,1152]{1,0:T(8,128)(2,1)} %embed_ref.3, bf16[1728,1152]{1,0:T(8,128)(2,1)} %bitcast.19, bf16[576,1152]{1,0:T(8,128)(2,1)} %output_ref.3), custom_call_target="tpu_custom_call" | custom-call | flops 13589544960 | bytes 16072704 | tf_op jit(solution)/shard_map/space_block/pallas_call | solution.py:245
  29.1 35.0 %time_block.2 = (f32[16,16,128]{2,1,0:T(8,128)}, bf16[16,16,128]{2,1,0:T(8,128)(2,1)}) custom-call(s32[1]{0:T(128)} %bitcast.step_ref.refs_0_, bf16[16,128,1152]{2,1,0:T(8,128)(2,1)} %space_block.2.refs_1_, f32[16,8,1152]{2,1,0:T(8,128)} %refs_2_.3, bf16[1728,1152]{1,0:T(8,128)(2,1)} %bitcast.21, bf16[576,1152]{1,0:T(8,128)(2,1)} %refs_4_.3, ...), custom_call_target="tpu_custom_call" | custom-call | flops 13589544960 | bytes 16072704 | tf_op jit(solution)/shard_map/time_block/pallas_call | solution.py:278
  64.1 13.6 %carry.1.latent_ref = f32[256,128]{1,0:T(8,128)} custom-call(bf16[256,128]{1,0:T(8,128)(2,1)} %bitcast.18, f32[256,128]{1,0:T(8,128)} %bitcast.16, f32[256,128]{1,0:T(8,128)} %bitcast.14), custom_call_target="tpu_custom_call" | custom-call | tf_op jit(solution)/shard_map/carry/pallas_call | solution.py:424
  77.7 29.1 %space_block.3.refs_1_ = bf16[16,128,1152]{2,1,0:T(8,128)(2,1)} custom-call(s32[1]{0:T(128)} %bitcast.step_ref.refs_0_, f32[16,16,128]{2,1,0:T(8,128)} %bitcast.11, f32[16,8,1152]{2,1,0:T(8,128)} %refs_2_.3, bf16[16,1152]{1,0:T(8,128)(2,1)} %embed_ref.3, bf16[1728,1152]{1,0:T(8,128)(2,1)} %bitcast.20, bf16[576,1152]{1,0:T(8,128)(2,1)} %output_ref.3), custom_call_target="tpu_custom_call" | custom-call | flops 13589544960 | bytes 16072704 | tf_op jit(solution)/shard_map/space_block/pallas_call | solution.py:245
  106.8 35.0 %time_block.3 = (f32[16,16,128]{2,1,0:T(8,128)}, bf16[16,16,128]{2,1,0:T(8,128)(2,1)}) custom-call(s32[1]{0:T(128)} %bitcast.step_ref.refs_0_, bf16[16,128,1152]{2,1,0:T(8,128)(2,1)} %space_block.3.refs_1_, f32[16,8,1152]{2,1,0:T(8,128)} %refs_2_.3, bf16[1728,1152]{1,0:T(8,128)(2,1)} %bitcast.22, bf16[576,1152]{1,0:T(8,128)(2,1)} %refs_4_.3, ...), custom_call_target="tpu_custom_call" | custom-call | flops 13589544960 | bytes 16072704 | tf_op jit(solution)/shard_map/time_block/pallas_call | solution.py:278
  141.8 13.4 %carry_last.1 = f32[256,128]{1,0:T(8,128)} custom-call(bf16[256,128]{1,0:T(8,128)(2,1)} %bitcast.17, f32[256,128]{1,0:T(8,128)} %bitcast.15, f32[256,128]{1,0:T(8,128)} %carry.1.latent_ref), custom_call_target="tpu_custom_call" | custom-call | tf_op jit(solution)/shard_map/carry_last/pallas_call | solution.py:424
  155.2 1.6 %copy.14 = f32[16,16,128]{2,1,0:T(8,128)} copy(f32[16,16,128]{2,1,0:T(8,128)} %bitcast.13) | data formatting | bytes 262144
